TPU v7x, 32 devices: a whole 2x2x4 slice. The times are simulated.
32 devices in a mesh: lat: 2 (over core), prop: 16 (over z, y, x).
Axes of the slice: x: 2, y: 2, z: 4, core: 2. Of those that a mesh axis runs over, the one named last changes fastest.
Arguments:
- right_side: float32 [2, 3, 16, 64, 4, 128], P(None, None, None, 'prop', 'lat'), may hold values from -30 to 30
- start_field: float32 [2, 3, 16, 64, 4, 128], P(None, None, None, 'prop', 'lat'), may hold values from -1.75 to 1.75
- region: int32 [64, 4, 128], P('prop', 'lat'), may hold values from 0 to 7
- core_mask: int32 [64, 4, 128], P('prop', 'lat'), may hold values 0 or 1
- intensity: float32 [64, 4, 128], P('prop', 'lat'), may hold values from 0 to 4
- eps_lin: float32 [8], replicated, may hold values from 1 to 12
- eps_loss: float32 [8], replicated, may hold values from 0.1 to 3
- kerr_coef: float32 [8], replicated, may hold values from 0.2 to 1
Outputs:
- new_field: float32 [2, 3, 16, 64, 4, 128], P(None, None, None, 'prop', 'lat')
All inputs are finite; a program needn't handle non-finite values. No bound on the sum of `core_mask` on one device may be relied on, other than what follows from the above.
Results may differ from a plain program's by a relative error of at most 0.00002.
Values sent between devices are 32-bit elements; how exact they have to be, the bound alone decides.
A program may use at most 64 MiB of HBM per device.

v0:
```python
import jax
import jax.numpy as jnp
from jax import lax
from jax.sharding import PartitionSpec as P

wave_sq = 0.25
wave_shift = 0.02
loss_gain = 3.2
tiny = 1e-06


def extended(array, sides, width):
    for axis, dim in sides:
        size, length = (lax.axis_size(axis), array.shape[dim])
        up = [(i, (i + 1) % size) for i in range(size - 1)]
        down = [(j, i) for i, j in up]
        last = lax.slice_in_dim(array, length - width, length, axis=dim)
        first = lax.slice_in_dim(array, 0, width, axis=dim)
        before = lax.ppermute(last, axis, up)
        after = lax.ppermute(first, axis, down)
        array = jnp.concatenate([before, array, after], axis=dim)
    return array


def trimmed(values, direction):
    selector = [slice(None)] * (values.ndim - 3) + [slice(0, -1)] * 3
    if direction is not None:
        selector[values.ndim + direction] = slice(1, None)
    return values[tuple(selector)]


def advance(values, direction):
    return trimmed(values, direction) - trimmed(values, None)


def upper(values, direction):
    selector = [slice(None)] * (values.ndim - 3) + [slice(1, None)] * 3
    if direction is not None:
        selector[values.ndim + direction] = slice(0, -1)
    return values[tuple(selector)]


def retreat(values, direction):
    return upper(values, None) - upper(values, direction)


def curl_twice(padded):
    field_x = padded[:, 0]
    field_y = padded[:, 1]
    field_z = padded[:, 2]
    magnet_x = advance(field_z, -1) - advance(field_y, -3)
    magnet_y = advance(field_x, -3) - advance(field_z, -2)
    magnet_z = advance(field_y, -2) - advance(field_x, -1)
    result_x = retreat(magnet_z, -1) - retreat(magnet_y, -3)
    result_y = retreat(magnet_x, -3) - retreat(magnet_z, -2)
    result_z = retreat(magnet_y, -2) - retreat(magnet_x, -1)
    return jnp.stack([result_x, result_y, result_z], axis=1)


def apply_operator(values, padded, perm_real, perm_imag):
    curled = curl_twice(padded)
    real_part = values[0]
    imag_part = values[1]
    out_real = curled[0] - wave_sq * (perm_real * real_part - perm_imag * imag_part)
    out_imag = curled[1] - wave_sq * (perm_real * imag_part + perm_imag * real_part)
    return jnp.stack([out_real, out_imag])


def ascend(gain_real, gain_imag, forward_value, behind):
    return jnp.stack(
        [
            forward_value[0] + gain_real * behind[0] - gain_imag * behind[1],
            forward_value[1] + gain_real * behind[1] + gain_imag * behind[0],
        ]
    )


def solve_batched(line_data, diag_real, diag_imag):
    depth = line_data.shape[3]
    lines_count = line_data.shape[4] * line_data.shape[5]
    moved = jnp.moveaxis(line_data, 3, 0)
    moved_shape = moved.shape
    rows = moved.reshape((depth, 2, -1))
    repeats = rows.shape[2] // lines_count
    plane_real = diag_real.reshape((depth, lines_count))
    plane_imag = diag_imag.reshape((depth, lines_count))
    unroll_count = min(16, depth)

    def gain_step(carried, element):
        gain_real, gain_imag = carried
        diag_now_real, diag_now_imag = element
        denom_real = diag_now_real - gain_real
        denom_imag = diag_now_imag - gain_imag
        magnitude = denom_real * denom_real + denom_imag * denom_imag
        new_real = denom_real / magnitude
        new_imag = -denom_imag / magnitude
        return ((new_real, new_imag), (new_real, new_imag))

    zero_line = jnp.zeros((lines_count,), jnp.float32)
    unused, (gains_real, gains_imag) = lax.scan(
        gain_step, (zero_line, zero_line), (plane_real, plane_imag), unroll=unroll_count
    )
    wide_real = jnp.tile(gains_real, (1, repeats))
    wide_imag = jnp.tile(gains_imag, (1, repeats))

    def front_step(previous, element):
        gain_real, gain_imag, source = element
        sum_real = source[0] + previous[0]
        sum_imag = source[1] + previous[1]
        updated = jnp.stack(
            [
                gain_real * sum_real - gain_imag * sum_imag,
                gain_real * sum_imag + gain_imag * sum_real,
            ]
        )
        return (updated, updated)

    unused, fronts = lax.scan(
        front_step, jnp.zeros_like(rows[0]), (wide_real, wide_imag, rows), unroll=unroll_count
    )

    def back_step(behind, element):
        gain_real, gain_imag, forward_value = element
        new_value = ascend(gain_real, gain_imag, forward_value, behind)
        return (new_value, new_value)

    unused, values = lax.scan(
        back_step,
        jnp.zeros_like(rows[0]),
        (wide_real, wide_imag, fronts),
        reverse=True,
        unroll=unroll_count,
    )
    return jnp.moveaxis(values.reshape(moved_shape), 0, 3)


def per_device(right_side, start_field, region, core_mask, intensity, eps_lin, eps_loss, kerr_coef):
    levels = jnp.arange(eps_lin.shape[0], dtype=jnp.int32)
    onehot = (region[None] == levels[:, None, None, None]).astype(jnp.float32)
    lin_cell = jnp.sum(onehot * eps_lin[:, None, None, None], axis=0)
    loss_cell = jnp.sum(onehot * eps_loss[:, None, None, None], axis=0)
    kerr_cell = jnp.sum(onehot * kerr_coef[:, None, None, None], axis=0)
    perm_real = lin_cell + core_mask.astype(jnp.float32) * kerr_cell * intensity
    planes = right_side.shape[3]
    total_planes = planes * lax.axis_size("prop")
    diag_real = 2.0 - wave_shift * perm_real
    diag_imag = loss_gain / total_planes * loss_cell

    def operate(values):
        padded = extended(values, (("lat", 4), ("prop", 3)), 1)
        padded = jnp.pad(padded, ((0, 0), (0, 0), (0, 0), (0, 0), (0, 0), (1, 1)))
        return apply_operator(values, padded, perm_real, loss_cell)

    residual = right_side - operate(start_field)
    coeffs = jnp.stack([diag_real, diag_imag])
    line_diag = lax.all_to_all(coeffs, "prop", split_axis=3, concat_axis=1, tiled=True)
    solved = solve_batched(
        lax.all_to_all(residual, "prop", split_axis=5, concat_axis=3, tiled=True),
        line_diag[0],
        line_diag[1],
    )
    precond = lax.all_to_all(solved, "prop", split_axis=3, concat_axis=5, tiled=True)
    image_field = operate(precond)
    cross_sum = jnp.sum(residual * image_field, axis=(0, 1, 3, 4, 5))
    self_sum = jnp.sum(image_field * image_field, axis=(0, 1, 3, 4, 5))
    totals = lax.psum((cross_sum, self_sum), ("lat", "prop"))
    step_size = totals[0] / (totals[1] + tiny)
    return start_field + step_size[None, None, :, None, None, None] * precond


def solution(mesh):
    placed = (
        P(None, None, None, "prop", "lat", None),
        P(None, None, None, "prop", "lat", None),
        P("prop", "lat", None),
        P("prop", "lat", None),
        P("prop", "lat", None),
        P(),
        P(),
        P(),
    )
    return jax.shard_map(
        per_device,
        mesh=mesh,
        in_specs=placed,
        out_specs=P(None, None, None, "prop", "lat", None),
        check_vma=False,
    )
```

profile of v0, /device:TPU:0, one launch (start us, length us, event | category | flops | bytes accessed | tf_op | source)
XLA Modules:
  0.0 232.1 jit_solution(9379006360073458968)
XLA Ops:
  1.2 2.4 %collective-permute-start = (f32[2,3,16,4,1,128]{5,2,4,3,1,0:T(8,128)S(1)}, f32[2,3,16,4,1,128]{5,2,4,3,1,0:T(8,128)S(1)}, u32[]{:S(2)}, u32[]{:S(2)}) collective-permute-start(f32[2,3,16,4,1,128]{5,2,4,3,1,0:T(8,128)S(1)} %get-tuple-element.468), channel_id=1, source_target_pairs={{0,16},{1,17},{2,18},{3,19},{4,20},{5,21},{6,22},{7,23},{8,24},{9,... | collective-permute-start | bytes 589832 | tf_op jit(solution)/shard_map/ppermute | solution.py:19
  6.3 7.7 %all-to-all-start = ((f32[16,1,128]{2,1,0:T(1,128)}), f32[16,1,128]{2,1,0:T(1,128)S(1)}, u32[]{:S(2)}, u32[]{:S(2)}) async-start(f32[16,1,128]{2,1,0:T(1,128)} %reshape.3988), calls=%async_computation | async-start | bytes 16384 | tf_op jit(solution)/shard_map/all_to_all | solution.py:156
  15.3 5.9 %all-to-all-done = f32[16,1,128]{2,1,0:T(1,128)S(1)} async-done(((f32[16,1,128]{2,1,0:T(1,128)}), f32[16,1,128]{2,1,0:T(1,128)S(1)}, u32[]{:S(2)}, u32[]{:S(2)}) %all-to-all-start) | async-done | bytes 8224 | tf_op jit(solution)/shard_map/all_to_all | solution.py:156
  23.6 2.5 %collective-permute-start.2 = (f32[2,3,16,1,4,128]{5,2,4,3,1,0:T(8,128)S(1)}, f32[2,3,16,1,4,128]{5,2,4,3,1,0:T(8,128)S(1)}, u32[]{:S(2)}, u32[]{:S(2)}) collective-permute-start(f32[2,3,16,1,4,128]{5,2,4,3,1,0:T(8,128)S(1)} %get-tuple-element.459), channel_id=1, source_target_pairs={{0,1},{1,2},{2,3},{3,4},{4,5},{5,6},{6,7},{7,8},{8,9},{9,10},{10,1... | collective-permute-start | bytes 589832 | tf_op jit(solution)/shard_map/ppermute | solution.py:19
  29.3 5.3 %collective-permute-done.3 = f32[2,3,16,1,4,128]{5,2,4,3,1,0:T(8,128)S(1)} collective-permute-done((f32[2,3,16,1,4,128]{5,2,4,3,1,0:T(8,128)S(1)}, f32[2,3,16,1,4,128]{5,2,4,3,1,0:T(8,128)S(1)}, u32[]{:S(2)}, u32[]{:S(2)}) %collective-permute-start.3) | collective-permute-done | bytes 196640 | tf_op jit(solution)/shard_map/ppermute | solution.py:20
  37.1 2.2 copy.238
  39.4 4.9 %reshape.3990 = f32[16,1,6144]{2,1,0:T(1,128)} reshape(f32[128,2,3,4,2,16]{5,4,3,2,1,0:T(2,128)S(1)} %bitcast.1633) | data formatting | bytes 786432
  44.2 4.6 %all-to-all-start.1 = ((f32[16,1,6144]{2,1,0:T(1,128)}), f32[16,1,6144]{2,1,0:T(1,128)S(1)}, u32[]{:S(2)}, u32[]{:S(2)}) async-start(f32[16,1,6144]{2,1,0:T(1,128)} %reshape.3990), calls=%async_computation.1 | async-start | bytes 786432 | tf_op jit(solution)/shard_map/all_to_all | solution.py:158
  48.9 44.4 %while.47 = (s32[]{:T(128)}, f32[16]{0:T(128)S(1)}, f32[16]{0:T(128)S(1)}, f32[4,16,16]{2,1,0:T(8,128)S(1)}, f32[4,16,16]{2,1,0:T(8,128)S(1)}, /*index=5*/f32[4,...) while((s32[]{:T(128)}, f32[16]{0:T(128)S(1)}, ...), condition=%wide.region_4.5_spmd.clone, body=%wide.region_3.4_spmd.clone.sunk | while | flops 2482 | bytes 45483 | solution.py:100
  94.9 2.4 %reduce.1 = f32[16,6144]{1,0:T(8,128)} reduce(f32[16,1,6144]{2,1,0:T(1,128)S(1)} %all-to-all-done.1, f32[]{:T(128)} %broadcast.160), dimensions={1}, to_apply=%all_to_all.40.reduce_sub_computation | reduce | bytes 786436 | tf_op jit(solution)/shard_map/all_to_all | solution.py:158
  97.2 5.3 %reshape.3991 = f32[128,2,3,4,2,16]{5,4,3,2,1,0:T(2,128)S(1)} reshape(f32[16,6144]{1,0:T(8,128)} %reduce.1) | data formatting | bytes 786432
  103.9 2.3 copy.241
  106.1 2.5 %reshape_reshape.6 = f32[4,16,2,768]{1,0,3,2:T(4,128)S(1)} reshape(f32[64,2,3,16,2,8]{0,5,4,3,2,1:T(8,128)} %copy.241) | data formatting | bytes 786432 | tf_op jit(solution)/shard_map/reshape;reshape | solution.py:118
  108.7 2.1 copy.242
  110.9 9.7 %while.45 = (s32[]{:T(128)}, f32[2,768]{1,0:T(2,128)S(1)}, f32[4,16,2,768]{3,2,1,0:T(2,128)S(1)}, f32[4,16,768]{2,1,0:T(8,128)S(1)}, f32[4,16,2,768]{3,2,1,0:T(2...) while((s32[]{:T(128)}, f32[2,768]{1,0:T(2,128)S(1)}, ...), condition=%wide.region_6.7_spmd, body=%wide.region_5.6_spmd.sunk | while | flops 124432 | bytes 719313 | solution.py:118
  120.7 2.9 %while.46 = (s32[]{:T(128)}, f32[2,768]{1,0:T(2,128)S(1)}, f32[4,16,2,768]{3,2,1,0:T(2,128)S(1)}, f32[4,16,2,768]{3,2,1,0:T(2,128)S(1)}, f32[4,16,768]{2,1,0:T(8...) while((s32[]{:T(128)}, f32[2,768]{1,0:T(2,128)S(1)}, ...), condition=%wide.region_8.9_spmd, body=%wide.region_7.8_spmd.sunk | while | flops 122897 | bytes 713185 | solution.py:127
  124.4 2.8 %copy.243 = f32[4,16,2,768]{1,0,3,2:T(4,128)S(1)} copy(f32[4,16,2,768]{3,2,1,0:T(2,128)} %copy-done.8) | data formatting | bytes 786432 | tf_op jit(solution)/shard_map/while | solution.py:127
  127.2 2.2 reshape_reshape.7
  129.4 2.7 %copy.244 = f32[2,3,16,64,2,8]{2,5,4,1,0,3:T(8,128)S(1)} copy(f32[2,3,16,64,2,8]{3,5,4,2,1,0:T(8,128)} %bitcast.1638) | data formatting | bytes 786432 | tf_op jit(solution)/shard_map/transpose | solution.py:134
  133.2 18.1 %all_to_all.51 = f32[16,1,6144]{2,1,0:T(1,128)S(1)} all-to-all(f32[16,1,6144]{2,1,0:T(1,128)S(1)} %reshape.3992), channel_id=1, replica_groups=mesh['lat'=2,'prop'=16] {'prop'}, dimensions={0} | all-to-all | bytes 786432 | tf_op jit(solution)/shard_map/all_to_all | solution.py:162
  153.9 2.1 copy.245
  156.6 2.3 copy.279
  158.9 1.9 fusion.385
  161.9 2.7 %copy.247 = f32[2,3,16,4,1,128]{5,2,4,3,1,0:T(8,128)} copy(f32[2,3,16,4,1,128]{2,5,4,3,1,0:T(8,128)} %get-tuple-element.439) | data formatting | bytes 393216 | tf_op jit(solution)/shard_map/slice | solution.py:17
  164.6 2.0 collective-permute-start.4
  166.5 2.5 %copy.248 = f32[2,3,16,4,1,128]{5,2,4,3,1,0:T(8,128)} copy(f32[2,3,16,4,1,128]{2,5,4,3,1,0:T(8,128)} %get-tuple-element.440) | data formatting | bytes 393216 | tf_op jit(solution)/shard_map/slice | solution.py:18
  170.7 1.9 collective-permute-done.5
  172.6 1.7 pad_maximum_fusion.7
  174.3 3.2 %collective-permute-start.6 = (f32[2,3,16,1,4,128]{5,2,4,3,1,0:T(8,128)}, f32[2,3,16,1,4,128]{5,2,4,3,1,0:T(8,128)}, u32[]{:S(2)}, u32[]{:S(2)}) collective-permute-start(f32[2,3,16,1,4,128]{5,2,4,3,1,0:T(8,128)} %get-tuple-element.454), channel_id=1, source_target_pairs={{0,1},{1,2},{2,3},{3,4},{4,5},{5,6},{6,7},{7,8},{8,9},{9,10},{10,1... | collective-permute-start | bytes 589832 | tf_op jit(solution)/shard_map/ppermute | solution.py:19
  181.5 6.4 %collective-permute-done.7 = f32[2,3,16,1,4,128]{5,2,4,3,1,0:T(8,128)} collective-permute-done((f32[2,3,16,1,4,128]{5,2,4,3,1,0:T(8,128)}, f32[2,3,16,1,4,128]{5,2,4,3,1,0:T(8,128)}, u32[]{:S(2)}, u32[]{:S(2)}) %collective-permute-start.7) | collective-permute-done | bytes 196640 | tf_op jit(solution)/shard_map/ppermute | solution.py:20
  187.9 1.9 select_maximum_fusion
  192.0 39.1 %all-reduce.2 = (f32[16]{0:T(128)S(1)}, f32[16]{0:T(128)S(1)}) all-reduce(f32[16]{0:T(128)S(1)} %get-tuple-element.262, f32[16]{0:T(128)S(1)} %get-tuple-element.261), channel_id=1, replica_groups=mesh['lat'=2,'prop'=16] {'lat','prop'}, use_global_device_ids=true, to_apply=%region_10.11 | all-reduce | flops 32 | bytes 256 | tf_op jit(solution)/shard_map/psum | solution.py:166
  (327 shorter events, 87.4 us)
Async XLA Ops:
  0.0 23.4 %copy-start.2 = (f32[2,3,16,4,2,128]{5,4,3,2,1,0:T(2,128)S(1)}, f32[2,3,16,4,2,128]{5,4,3,2,1,0:T(2,128)}, u32[]{:S(2)}) copy-start(f32[2,3,16,4,2,128]{5,4,3,2,1,0:T(2,128)} %param.15) | copy-start | bytes 1179652
  1.2 22.2 %collective-permute-start = (f32[2,3,16,4,1,128]{5,2,4,3,1,0:T(8,128)S(1)}, f32[2,3,16,4,1,128]{5,2,4,3,1,0:T(8,128)S(1)}, u32[]{:S(2)}, u32[]{:S(2)}) collective-permute-start(f32[2,3,16,4,1,128]{5,2,4,3,1,0:T(8,128)S(1)} %get-tuple-element.468), channel_id=1, source_target_pairs={{0,16},{1,17},{2,18},{3,19},{4,20},{5,21},{6,22},{7,23},{8,24},{9,... | collective-permute-start | bytes 589832 | tf_op jit(solution)/shard_map/ppermute | solution.py:19
  6.3 14.9 %all-to-all-start = ((f32[16,1,128]{2,1,0:T(1,128)}), f32[16,1,128]{2,1,0:T(1,128)S(1)}, u32[]{:S(2)}, u32[]{:S(2)}) async-start(f32[16,1,128]{2,1,0:T(1,128)} %reshape.3988), calls=%async_computation | async-start | bytes 16384 | tf_op jit(solution)/shard_map/all_to_all | solution.py:156
  14.0 9.5 %collective-permute-start.1 = (f32[2,3,16,4,1,128]{5,2,4,3,1,0:T(8,128)S(1)}, f32[2,3,16,4,1,128]{5,2,4,3,1,0:T(8,128)S(1)}, u32[]{:S(2)}, u32[]{:S(2)}) collective-permute-start(f32[2,3,16,4,1,128]{5,2,4,3,1,0:T(8,128)S(1)} %get-tuple-element.467), channel_id=1, source_target_pairs={{16,0},{17,1},{18,2},{19,3},{20,4},{21,5},{22,6},{23,7},{24,8},{25... | collective-permute-start | bytes 589832 | tf_op jit(solution)/shard_map/ppermute | solution.py:20
  23.6 5.7 %collective-permute-start.2 = (f32[2,3,16,1,4,128]{5,2,4,3,1,0:T(8,128)S(1)}, f32[2,3,16,1,4,128]{5,2,4,3,1,0:T(8,128)S(1)}, u32[]{:S(2)}, u32[]{:S(2)}) collective-permute-start(f32[2,3,16,1,4,128]{5,2,4,3,1,0:T(8,128)S(1)} %get-tuple-element.459), channel_id=1, source_target_pairs={{0,1},{1,2},{2,3},{3,4},{4,5},{5,6},{6,7},{7,8},{8,9},{9,10},{10,1... | collective-permute-start | bytes 589832 | tf_op jit(solution)/shard_map/ppermute | solution.py:19
  26.1 8.5 %collective-permute-start.3 = (f32[2,3,16,1,4,128]{5,2,4,3,1,0:T(8,128)S(1)}, f32[2,3,16,1,4,128]{5,2,4,3,1,0:T(8,128)S(1)}, u32[]{:S(2)}, u32[]{:S(2)}) collective-permute-start(f32[2,3,16,1,4,128]{5,2,4,3,1,0:T(8,128)S(1)} %get-tuple-element.460), channel_id=1, source_target_pairs={{1,0},{2,1},{3,2},{4,3},{5,4},{6,5},{7,6},{8,7},{9,8},{10,9},{11,1... | collective-permute-start | bytes 589832 | tf_op jit(solution)/shard_map/ppermute | solution.py:20
  35.8 1.2 copy-start.9
  36.3 0.7 copy-start.4
  36.3 0.7 copy-start.6
  39.3 9.6 %copy-start.13 = (f32[4,16,16]{2,1,0:T(8,128)S(1)}, f32[4,16,16]{2,1,0:T(8,128)}, u32[]{:S(2)}) copy-start(f32[4,16,16]{2,1,0:T(8,128)} %custom-call.5) | copy-start | bytes 12292
  39.3 9.6 %copy-start.14 = (f32[4,16,16]{2,1,0:T(8,128)S(1)}, f32[4,16,16]{2,1,0:T(8,128)}, u32[]{:S(2)}) copy-start(f32[4,16,16]{2,1,0:T(8,128)} %custom-call.6) | copy-start | bytes 12292
  44.2 50.6 %all-to-all-start.1 = ((f32[16,1,6144]{2,1,0:T(1,128)}), f32[16,1,6144]{2,1,0:T(1,128)S(1)}, u32[]{:S(2)}, u32[]{:S(2)}) async-start(f32[16,1,6144]{2,1,0:T(1,128)} %reshape.3990), calls=%async_computation.1 | async-start | bytes 786432 | tf_op jit(solution)/shard_map/all_to_all | solution.py:158
  123.7 0.7 copy-start.8
  153.9 2.7 %copy-start = (f32[64,2,3,2,8,16]{5,4,3,2,1,0:T(8,128)}, f32[64,2,3,2,8,16]{5,4,3,2,1,0:T(8,128)S(1)}, u32[]{:S(2)}) copy-start(f32[64,2,3,2,8,16]{5,4,3,2,1,0:T(8,128)S(1)} %reshape.3993) | copy-start | bytes 1179652
  161.8 8.5 %copy-start.1 = (f32[2,3,16,64,2,8]{2,5,4,3,1,0:T(8,128)S(1)}, f32[2,3,16,64,2,8]{2,5,4,3,1,0:T(8,128)}, u32[]{:S(2)}) copy-start(f32[2,3,16,64,2,8]{2,5,4,3,1,0:T(8,128)} %copy.245) | copy-start | bytes 1179652
  164.6 6.2 %collective-permute-start.4 = (f32[2,3,16,4,1,128]{5,2,4,3,1,0:T(8,128)}, f32[2,3,16,4,1,128]{5,2,4,3,1,0:T(8,128)}, u32[]{:S(2)}, u32[]{:S(2)}) collective-permute-start(f32[2,3,16,4,1,128]{5,2,4,3,1,0:T(8,128)} %copy.247), channel_id=1, source_target_pairs={{0,16},{1,17},{2,18},{3,19},{4,20},{5,21},{6,22},{7,23},{8,24},{9,... | collective-permute-start | bytes 589832 | tf_op jit(solution)/shard_map/ppermute | solution.py:19
  169.1 3.5 %collective-permute-start.5 = (f32[2,3,16,4,1,128]{5,2,4,3,1,0:T(8,128)}, f32[2,3,16,4,1,128]{5,2,4,3,1,0:T(8,128)S(1)}, u32[]{:S(2)}, u32[]{:S(2)}) collective-permute-start(f32[2,3,16,4,1,128]{5,2,4,3,1,0:T(8,128)} %copy.248), channel_id=1, source_target_pairs={{16,0},{17,1},{18,2},{19,3},{20,4},{21,5},{22,6},{23,7},{24,8},{25... | collective-permute-start | bytes 589832 | tf_op jit(solution)/shard_map/ppermute | solution.py:20
  172.6 6.5 %copy-start.12 = (f32[2,3,16,4,1,128]{5,2,4,3,1,0:T(8,128)}, f32[2,3,16,4,1,128]{5,2,4,3,1,0:T(8,128)S(1)}, u32[]{:S(2)}) copy-start(f32[2,3,16,4,1,128]{5,2,4,3,1,0:T(8,128)S(1)} %collective-permute-done.5) | copy-start | bytes 589828
  174.3 7.2 %collective-permute-start.6 = (f32[2,3,16,1,4,128]{5,2,4,3,1,0:T(8,128)}, f32[2,3,16,1,4,128]{5,2,4,3,1,0:T(8,128)}, u32[]{:S(2)}, u32[]{:S(2)}) collective-permute-start(f32[2,3,16,1,4,128]{5,2,4,3,1,0:T(8,128)} %get-tuple-element.454), channel_id=1, source_target_pairs={{0,1},{1,2},{2,3},{3,4},{4,5},{5,6},{6,7},{7,8},{8,9},{9,10},{10,1... | collective-permute-start | bytes 589832 | tf_op jit(solution)/shard_map/ppermute | solution.py:19
  177.4 10.5 %collective-permute-start.7 = (f32[2,3,16,1,4,128]{5,2,4,3,1,0:T(8,128)}, f32[2,3,16,1,4,128]{5,2,4,3,1,0:T(8,128)}, u32[]{:S(2)}, u32[]{:S(2)}) collective-permute-start(f32[2,3,16,1,4,128]{5,2,4,3,1,0:T(8,128)} %get-tuple-element.455), channel_id=1, source_target_pairs={{1,0},{2,1},{3,2},{4,3},{5,4},{6,5},{7,6},{8,7},{9,8},{10,9},{11,1... | collective-permute-start | bytes 589832 | tf_op jit(solution)/shard_map/ppermute | solution.py:20
  190.4 0.9 copy-start.11
  190.4 1.0 copy-start.5
  190.4 1.1 copy-start.7
  190.4 1.3 copy-start.10
  190.5 40.6 %copy-start.3 = (f32[2,3,16,4,2,128]{5,4,3,2,1,0:T(2,128)S(1)}, f32[2,3,16,4,2,128]{5,4,3,2,1,0:T(2,128)}, u32[]{:S(2)}) copy-start(f32[2,3,16,4,2,128]{5,4,3,2,1,0:T(2,128)} %param.15) | copy-start | bytes 1179652
where the time goes:
time: 236 us; the launch traced here: 232 us
  other arithmetic  67.8 us (29%)
  local copies, waits for them, and re-layouts  57.5 us (24%)
  blocking collectives  57.2 us (24%)
  starting transfers between devices  27.5 us (12%)
  waiting for transfers between devices  20.6 us (9%)
    psum x1, blocking collectives, per_device(): totals = lax.psum((cross_sum, self_sum), ('lat', 'prop'))  39.1 us
    sub x28, other arithmetic, gain_step(): denom_imag = diag_now_imag - gain_imag  21.5 us
    sub x28, other arithmetic, gain_step(): denom_real = diag_now_real - gain_real  19.4 us
    all_to_all x1, blocking collectives, per_device(): lax.all_to_all(solved, 'prop', split_axis=3, concat_axis=5, tiled=True)  18.1 us
    unnamed x39, local copies, waits for them, and re-layouts  17.8 us
    ppermute x4, waiting for transfers between devices, extended(): after = lax.ppermute(first, axis, down)  13.6 us
    ppermute x4, starting transfers between devices, extended(): before = lax.ppermute(last, axis, up)  10 us
    all_to_all x1, starting transfers between devices, per_device(): lax.all_to_all(coeffs, 'prop', split_axis=3, concat_axis=1, tiled=True)  7.69 us
  transfers between devices with their start and end apart: 10, of which 6 were waited for; matrix products, arithmetic and copies ran while one was open for 25% of the time, Pallas kernels for 0%

commit v1 on v0

v1 whole, which is shorter than its diff:
```python
import functools

import jax
import jax.numpy as jnp
from jax import lax
from jax.experimental import pallas as pl
from jax.experimental.pallas import tpu as pltpu
from jax.sharding import PartitionSpec as P

MESH = pl.DeviceIdType.MESH
wave_sq = 0.25
wave_shift = 0.02
loss_gain = 3.2
tiny = 1e-06


def cmul(a, b):
    return (a[0] * b[0] - a[1] * b[1], a[0] * b[1] + a[1] * b[0])


def cadd(a, b):
    return (a[0] + b[0], a[1] + b[1])


def cinv(a):
    scale = 1.0 / (a[0] * a[0] + a[1] * a[1])
    return (a[0] * scale, -a[1] * scale)


def kernel(
    dims, lin_ref, loss_ref, kerr_ref, region_ref, mask_ref, inten_ref, rhs_ref, start_ref, out_ref,
    field, resid, local, pre, cell, corner, corner_all, link, tips_out, tips_in, ends_out, ends_in, part,
    lat_parts, prop_parts,
    halo_send, halo_recv, corner_send, corner_recv, tips_send, tips_recv, ends_send, ends_recv,
    pre_send, pre_recv, lat_send, lat_recv, prop_send, prop_recv,
):
    n, nl, S, Z, X, NY, u, m, rows = dims
    NREG = lin_ref.shape[0]
    lat = lax.axis_index("lat")
    prop = lax.axis_index("prop")
    has_up, has_down = prop + 1 < n, prop > 0
    has_right, has_left = lat + 1 < nl, lat > 0
    ZX = Z * X

    def at_prop(q):
        return {"lat": lat, "prop": q}

    def at(l, q):
        return {"lat": l, "prop": q}

    def others(count, me, act):
        def body(j, carry):
            act(lax.rem(me + j, count))
            return carry

        lax.fori_loop(1, count, body, 0)

    barrier = pltpu.get_barrier_semaphore()

    def greet(l, q):
        pl.semaphore_signal(barrier, inc=1, device_id=at(l, q), device_id_type=MESH)

    diag_up = jnp.logical_and(has_left, has_up)
    diag_down = jnp.logical_and(has_right, has_down)
    others(n, prop, lambda q: greet(lat, q))
    others(nl, lat, lambda l: greet(l, prop))
    pl.when(diag_up)(lambda: greet(lat - 1, prop + 1))
    pl.when(diag_down)(lambda: greet(lat + 1, prop - 1))

    zero_plane = jnp.zeros((X, S, NY), jnp.float32)
    zero_line = jnp.zeros((S, NY), jnp.float32)
    for c in range(2):
        for k in range(3):
            for z in range(Z):
                for x in range(X):
                    base = (c * 3 + k) * S * ZX + z * X + x
                    field[c, k, z + 1, x + 1] = start_ref[pl.ds(base, S, stride=ZX), :]

    def clear(cond, buf, planes, xs):
        @pl.when(cond)
        def _():
            for c in range(2):
                for k in range(3):
                    for z in planes:
                        for x in xs:
                            buf[c, k, z, x] = zero_line

    no_up, no_down = jnp.logical_not(has_up), jnp.logical_not(has_down)
    no_right, no_left = jnp.logical_not(has_right), jnp.logical_not(has_left)
    inner_z, inner_x = range(1, Z + 1), range(1, X + 1)
    for buf, wide in ((field, inner_z), (pre, range(Z + 2))):
        clear(no_left, buf, wide, (0,))
        clear(no_right, buf, wide, (X + 1,))
    clear(no_down, field, (0,), inner_x)
    clear(no_up, field, (Z + 1,), inner_x)
    clear(jnp.logical_or(no_down, no_right), field, (0,), (X + 1,))
    clear(jnp.logical_or(no_up, no_left), field, (Z + 1,), (0,))

    region = region_ref[...]
    lin = jnp.zeros((Z, X, NY), jnp.float32)
    loss = lin
    kerr = lin
    for r in range(NREG):
        hit = region == r
        lin = jnp.where(hit, lin_ref[r], lin)
        loss = jnp.where(hit, loss_ref[r], loss)
        kerr = jnp.where(hit, kerr_ref[r], kerr)
    perm_real = lin + mask_ref[...].astype(jnp.float32) * kerr * inten_ref[...]
    diag_real = 2.0 - wave_shift * perm_real
    diag_imag = loss_gain / (Z * n) * loss
    gains = []
    for z in range(Z):
        d = (diag_real[z], diag_imag[z])
        if z:
            d = (d[0] - gains[-1][0], d[1] - gains[-1][1])
        gains.append(cinv(d))
    front = [gains[0]]
    for z in range(1, Z):
        front.append(cmul(gains[z], front[-1]))
    from_below = [front[-1]]
    from_above = [gains[-1]]
    for z in range(Z - 2, -1, -1):
        from_below.insert(0, cadd(front[z], cmul(gains[z], from_below[0])))
        from_above.insert(0, cmul(gains[z], from_above[0]))
    for z in range(Z):
        kinds = (wave_sq * perm_real[z], wave_sq * loss[z], *gains[z], *from_below[z], *from_above[z])
        for i, value in enumerate(kinds):
            for x in range(X):
                cell[i, z, x] = value[x : x + 1, :]
    triple = (*from_below[0], *from_below[-1], *from_above[-1])
    for x in range(X):
        for i, value in enumerate(triple):
            corner[x, i : i + 1, :] = value[x : x + 1, :]
        corner[x, 6:8, :] = jnp.zeros((2, NY), jnp.float32)

    count = (n - 1) + (nl - 1) + diag_up.astype(jnp.int32) + diag_down.astype(jnp.int32)
    pl.semaphore_wait(barrier, count)

    def remote(src, dst, send, recv, device):
        return pltpu.make_async_remote_copy(
            src_ref=src, dst_ref=dst, send_sem=send, recv_sem=recv, device_id=device, device_id_type=MESH
        )

    iz, ix = pl.ds(1, Z), pl.ds(1, X)
    halo = [
        (has_up, field.at[:, :, Z, ix], field.at[:, :, 0, ix], at(lat, prop + 1), has_down),
        (has_down, field.at[:, 0:2, 1, ix], field.at[:, 0:2, Z + 1, ix], at(lat, prop - 1), has_up),
        (diag_up, field.at[:, 2, Z, 1], field.at[:, 2, 0, X + 1], at(lat - 1, prop + 1), diag_down),
        (diag_down, field.at[:, 0, 1, X], field.at[:, 0, Z + 1, 0], at(lat + 1, prop - 1), diag_up),
        (has_right, field.at[:, :, iz, X], field.at[:, :, iz, 0], at(lat + 1, prop), has_left),
        (has_left, field.at[:, 1:3, iz, 1], field.at[:, 1:3, iz, X + 1], at(lat - 1, prop), has_right),
    ]
    halos = [
        (remote(src, dst, halo_send.at[i], halo_recv.at[i], device), out, into)
        for i, (out, src, dst, device, into) in enumerate(halo)
    ]
    for copy, out, _ in halos:
        pl.when(out)(copy.start)

    def corner_copy(q):
        return remote(corner.at[q // m], corner_all.at[prop], corner_send.at[q], corner_recv.at[prop], at_prop(q))

    others(n, prop, lambda q: corner_copy(q).start())
    corner_all[prop] = corner[prop // m]

    lane = lax.broadcasted_iota(jnp.int32, (X, S, NY), 2)
    at_first, at_last = lane == 0, lane == NY - 1

    def after(v):
        return jnp.where(at_last, 0.0, pltpu.roll(v, NY - 1, 2))

    def before(v):
        return jnp.where(at_first, 0.0, pltpu.roll(v, 1, 2))

    def curl(buf, c, z):
        def get(k, dz, dx):
            return buf[c, k, z + 1 + dz, 1 + dx : 1 + dx + X]

        ux, uy, uz = get(0, 0, 0), get(1, 0, 0), get(2, 0, 0)
        ux_up, uy_up = get(0, 1, 0), get(1, 1, 0)
        uz_down = get(2, -1, 0)
        uy_right, uz_right = get(1, 0, 1), get(2, 0, 1)
        ux_left = get(0, 0, -1)
        t = uy_right - uy
        out_x = (
            t + 4.0 * ux - after(ux) - before(ux + t) - get(0, -1, 0) - ux_up
            + (uz_right - uz) - (get(2, -1, 1) - uz_down)
        )
        ab = (uz - uz_down) + (ux - ux_left)
        out_y = 4.0 * uy - get(1, -1, 0) - uy_up - get(1, 0, -1) - uy_right + after(ab) - ab
        e = uy_up - uy
        out_z = (
            e + 4.0 * uz - after(uz) - before(uz + e) - get(2, 0, -1) - uz_right
            + (ux_up - ux) - (get(0, 1, -1) - ux_left)
        )
        return (out_x, out_y, out_z), (ux, uy, uz)

    def operate(buf, z):
        pr, pi = cell[0, z], cell[1, z]
        curl_re, re = curl(buf, 0, z)
        curl_im, im = curl(buf, 1, z)
        out_re = [curl_re[k] - (pr * re[k] - pi * im[k]) for k in range(3)]
        out_im = [curl_im[k] - (pr * im[k] + pi * re[k]) for k in range(3)]
        return out_re, out_im

    def residual(z):
        for c, parts in enumerate(operate(field, z)):
            for k in range(3):
                for x in range(X):
                    base = (c * 3 + k) * S * ZX + z * X + x
                    resid[c, k, z, x] = rhs_ref[pl.ds(base, S, stride=ZX), :] - parts[k][x]

    for i in (4, 5):
        pl.when(halos[i][2])(halos[i][0].wait_recv)
    for z in range(1, Z - 1):
        residual(z)
    for i in (0, 2):
        pl.when(halos[i][2])(halos[i][0].wait_recv)
    residual(0)
    for i in (1, 3):
        pl.when(halos[i][2])(halos[i][0].wait_recv)
    if Z > 1:
        residual(Z - 1)

    def coef(i, z):
        return (cell[i, z], cell[i + 1, z])

    def slot(base, b, c, k, a):
        return base + ((b * 2 + c) * 3 + k) * u + a

    for k in range(3):
        held = None
        for z in range(Z):
            r = (resid[0, k, z], resid[1, k, z])
            if held is not None:
                r = cadd(r, held)
            held = cmul(coef(2, z), r)
            if z < Z - 1:
                local[0, k, z] = held[0]
                local[1, k, z] = held[1]
        local[0, k, Z - 1], local[1, k, Z - 1] = held
        last = held
        for z in range(Z - 2, -1, -1):
            held = cadd((local[0, k, z], local[1, k, z]), cmul(coef(2, z), held))
            local[0, k, z], local[1, k, z] = held
        for b, ends in enumerate((held, last)):
            for c in range(2):
                for x in range(X):
                    for a in range(u):
                        tips_out[pl.ds(slot(x * m * rows, b, c, k, a), m, stride=rows), :] = ends[c][x, a * m : (a + 1) * m]

    def block(q):
        return pl.ds(pl.multiple_of(q * rows, 8), rows)

    def tips_copy(q):
        return remote(tips_out.at[block(q)], tips_in.at[block(prop)], tips_send.at[q], tips_recv.at[prop], at_prop(q))

    others(n, prop, lambda q: tips_copy(q).start())
    tips_in[block(prop), :] = tips_out[block(prop), :]

    def corner_from(q):
        return remote(corner.at[q // m], corner_all.at[q], corner_send.at[q], corner_recv.at[q], at_prop(q))

    others(n, prop, lambda q: corner_from(q).wait_recv())
    beta = (jnp.zeros((1, NY), jnp.float32),) * 2

    def link_step(k, beta):
        first, cross, last = [(corner_all[k, 2 * i : 2 * i + 1, :], corner_all[k, 2 * i + 1 : 2 * i + 2, :]) for i in range(3)]
        fb = cmul(first, beta)
        gamma = cinv((1.0 - fb[0], -fb[1]))
        carry = cmul(cross, gamma)
        mix = cmul(carry, beta)
        for i, value in enumerate((*carry, *mix, *gamma, *cmul(gamma, first), *beta)):
            link[k, i] = value
        return cadd(last, cmul(cross, mix))

    for k in range(n):
        beta = link_step(k, beta)

    def tips_from(q):
        return remote(tips_out.at[block(q)], tips_in.at[block(q)], tips_send.at[q], tips_recv.at[q], at_prop(q))

    others(n, prop, lambda q: tips_from(q).wait_recv())
    span = 3 * u

    def linked(k, i):
        return (link[k, 2 * i], link[k, 2 * i + 1])

    def tip(k, b):
        return tuple(tips_in[k * rows + (b * 2 + c) * span : k * rows + (b * 2 + c + 1) * span, :] for c in range(2))

    def put(k, b, value):
        for c in range(2):
            ends_out[k * rows + (b * 2 + c) * span : k * rows + (b * 2 + c + 1) * span, :] = value[c]

    none = (jnp.zeros((span, NY), jnp.float32),) * 2
    alphas = [none]
    for k in range(n):
        alphas.append(
            cadd(cadd(tip(k, 1), cmul(linked(k, 1), tip(k, 0))), cmul(linked(k, 0), alphas[-1]))
        )
    first = none
    for k in range(n - 1, -1, -1):
        put(k, 1, first)
        source = cadd(cmul(linked(k, 2), tip(k, 0)), cmul(linked(k, 3), alphas[k]))
        first = cadd(source, cmul(linked(k, 0), first))
        put(k, 0, cadd(alphas[k], cmul(linked(k, 4), first)) if k else none)

    def ends_copy(q):
        return remote(ends_out.at[block(q)], ends_in.at[block(prop)], ends_send.at[q], ends_recv.at[prop], at_prop(q))

    def ends_from(q):
        return remote(ends_out.at[block(q)], ends_in.at[block(q)], ends_send.at[q], ends_recv.at[q], at_prop(q))

    others(n, prop, lambda q: ends_copy(q).start())
    ends_in[block(prop), :] = ends_out[block(prop), :]
    others(n, prop, lambda q: ends_from(q).wait_recv())

    for k in range(3):
        sides = []
        for b in range(2):
            for c in range(2):
                for x in range(X):
                    for a in range(u):
                        pre[c, k, b * (Z + 1), 1 + x, a * m : (a + 1) * m, :] = ends_in[
                            pl.ds(slot(x * m * rows, b, c, k, a), m, stride=rows), :
                        ]
            sides.append(tuple(pre[c, k, b * (Z + 1), 1 : 1 + X] for c in range(2)))
        for z in range(Z):
            value = cadd((local[0, k, z], local[1, k, z]), cadd(cmul(coef(4, z), sides[0]), cmul(coef(6, z), sides[1])))
            for c in range(2):
                pre[c, k, z + 1, 1 : 1 + X] = value[c]
    side = [
        (has_right, pre.at[:, :, pl.ds(1, Z + 1), X], pre.at[:, :, pl.ds(1, Z + 1), 0], at(lat + 1, prop), has_left),
        (has_left, pre.at[:, 1:3, pl.ds(0, Z + 1), 1], pre.at[:, 1:3, pl.ds(0, Z + 1), X + 1], at(lat - 1, prop), has_right),
    ]
    sides = [
        (remote(src, dst, pre_send.at[i], pre_recv.at[i], device), out, into)
        for i, (out, src, dst, device, into) in enumerate(side)
    ]
    for copy, out, _ in sides:
        pl.when(out)(copy.start)
    for copy, _, into in sides:
        pl.when(into)(copy.wait_recv)

    cross_sum = zero_plane
    self_sum = zero_plane
    for z in range(Z):
        for c, parts in enumerate(operate(pre, z)):
            for k in range(3):
                cross_sum = cross_sum + resid[c, k, z] * parts[k]
                self_sum = self_sum + parts[k] * parts[k]
    column = lax.broadcasted_iota(jnp.int32, (S, NY), 0)
    place = lax.broadcasted_iota(jnp.int32, (S, NY), 1)
    on_cross, on_self = place == column, place == column + S
    totals = [jnp.sum(jnp.sum(v, axis=0), axis=1, keepdims=True) for v in (cross_sum, self_sum)]
    packed = jnp.where(on_cross, totals[0], jnp.where(on_self, totals[1], 0.0))
    row = jnp.sum(packed, axis=0, keepdims=True)

    def reduced(row, count, me, parts, i, send, recv, device):
        part[i] = row
        parts[me] = row

        def copy(q, own):
            return remote(part.at[i], parts.at[own], send.at[q], recv.at[own], device(q))

        others(count, me, lambda q: copy(q, me).start())
        others(count, me, lambda q: copy(q, q).wait_recv())
        others(count, me, lambda q: copy(q, q).wait_send())
        total = parts[0]
        for j in range(1, count):
            total = total + parts[j]
        return total

    row = reduced(row, nl, lat, lat_parts, 0, lat_send, lat_recv, lambda l: at(l, prop))
    row = reduced(row, n, prop, prop_parts, 1, prop_send, prop_recv, at_prop)
    wide = jnp.broadcast_to(row, (S, NY))
    cross_total = jnp.sum(jnp.where(on_cross, wide, 0.0), axis=1, keepdims=True)
    self_total = jnp.sum(jnp.where(on_self, wide, 0.0), axis=1, keepdims=True)
    size = jnp.broadcast_to(cross_total / (self_total + tiny), (S, NY))
    for c in range(2):
        for k in range(3):
            for z in range(Z):
                for x in range(X):
                    base = (c * 3 + k) * S * ZX + z * X + x
                    out_ref[pl.ds(base, S, stride=ZX), :] = field[c, k, z + 1, x + 1] + size * pre[c, k, z + 1, x + 1]
    for copy, out, _ in halos + sides:
        pl.when(out)(copy.wait_send)
    others(n, prop, lambda q: corner_from(q).wait_send())
    others(n, prop, lambda q: tips_from(q).wait_send())
    others(n, prop, lambda q: ends_from(q).wait_send())


def per_device(n, nl, right_side, start_field, region, core_mask, intensity, eps_lin, eps_loss, kerr_coef):
    S, Z, X, NY = right_side.shape[2:]
    m = n // X
    u = S // m
    rows = -(-12 * u // 8) * 8
    dims = (n, nl, S, Z, X, NY, u, m, rows)
    flat = (6 * S * Z * X, NY)
    f32 = jnp.float32
    vmem = pl.BlockSpec(memory_space=pltpu.VMEM)
    smem = pl.BlockSpec(memory_space=pltpu.SMEM)
    dma = pltpu.SemaphoreType.DMA
    out = pl.pallas_call(
        functools.partial(kernel, dims),
        out_shape=jax.ShapeDtypeStruct(flat, f32),
        in_specs=[smem] * 3 + [vmem] * 5,
        out_specs=vmem,
        scratch_shapes=[
            pltpu.VMEM((2, 3, Z + 2, X + 2, S, NY), f32),
            pltpu.VMEM((2, 3, Z, X, S, NY), f32),
            pltpu.VMEM((2, 3, Z, X, S, NY), f32),
            pltpu.VMEM((2, 3, Z + 2, X + 2, S, NY), f32),
            pltpu.VMEM((8, Z, X, 1, NY), f32),
            pltpu.VMEM((X, 8, NY), f32),
            pltpu.VMEM((n, 8, NY), f32),
            pltpu.VMEM((n, 10, 1, NY), f32),
            pltpu.VMEM((n * rows, NY), f32),
            pltpu.VMEM((n * rows, NY), f32),
            pltpu.VMEM((n * rows, NY), f32),
            pltpu.VMEM((n * rows, NY), f32),
            pltpu.VMEM((2, 1, NY), f32),
            pltpu.VMEM((nl, 1, NY), f32),
            pltpu.VMEM((n, 1, NY), f32),
            dma((6,)), dma((6,)),
            dma((n,)), dma((n,)),
            dma((n,)), dma((n,)),
            dma((n,)), dma((n,)),
            dma((2,)), dma((2,)),
            dma((nl,)), dma((nl,)),
            dma((n,)), dma((n,)),
        ],
        compiler_params=pltpu.CompilerParams(
            collective_id=0, has_side_effects=True, vmem_limit_bytes=32 * 1024 * 1024
        ),
    )(eps_lin, eps_loss, kerr_coef, region, core_mask, intensity, right_side.reshape(flat), start_field.reshape(flat))
    return out.reshape(right_side.shape)


def solution(mesh):
    placed = (
        P(None, None, None, "prop", "lat", None),
        P(None, None, None, "prop", "lat", None),
        P("prop", "lat", None),
        P("prop", "lat", None),
        P("prop", "lat", None),
        P(),
        P(),
        P(),
    )
    return jax.shard_map(
        functools.partial(per_device, mesh.shape["prop"], mesh.shape["lat"]),
        mesh=mesh,
        in_specs=placed,
        out_specs=P(None, None, None, "prop", "lat", None),
        check_vma=False,
    )
```

time: 236 us -> 40.8 us (0.17); the launches traced: 232 us -> 40.5 us
  other arithmetic: 67.8 us -> 0 us
  blocking collectives: 57.2 us -> 0 us
  local copies, waits for them, and re-layouts: 57.5 us -> 5.48 us
  Pallas kernels: 0 us -> 35 us
  starting transfers between devices: 27.5 us -> 0 us
  waiting for transfers between devices: 20.6 us -> 0 us
    sub x69 -> x0, other arithmetic: 48.2 us -> none  [the longest x28 21.5 us: gain_step(): denom_imag = diag_now_imag - gain_imag]
    psum x1 -> x0, blocking collectives: 39.1 us -> none  [per_device(): totals = lax.psum((cross_sum, self_sum), ('lat', 'prop'))]
    pallas_call x0 -> x1, Pallas kernels: none -> 35 us  [per_device(): pl.pallas_call(functools.partial(kernel, dims), out_shape=jax.ShapeDtypeS...]
    all_to_all x1 -> x0, blocking collectives: 18.1 us -> none  [per_device(): lax.all_to_all(solved, 'prop', split_axis=3, concat_axis=5, tiled=True)]
    ppermute x8 -> x0, starting transfers between devices: 15.2 us -> none  [the longest x4 10 us: extended(): before = lax.ppermute(last, axis, up)]
    ppermute x8 -> x0, waiting for transfers between devices: 14.8 us -> none  [the longest x4 13.6 us: extended(): after = lax.ppermute(first, axis, down)]
    all_to_all x2 -> x0, starting transfers between devices: 12.3 us -> none  [the longest x1 7.69 us: per_device(): lax.all_to_all(coeffs, 'prop', split_axis=3, concat_axis=1, tiled=True)]
    unnamed x39 -> x17, local copies, waits for them, and re-layouts: 17.8 us -> 5.48 us
  transfers between devices with their start and end apart: 10 -> 0, of which waited for: 6 -> 0; matrix products, arithmetic and copies ran while one was open for 25% -> 0% of each run, Pallas kernels for 0% -> 0%
where the time goes in v1:
time: 40.8 us; the launch traced here: 40.5 us
  Pallas kernels  35 us (86%)
  local copies, waits for them, and re-layouts  5.48 us (13%)
    pallas_call x1, Pallas kernels, per_device(): pl.pallas_call(functools.partial(kernel, dims), out_shape=jax.ShapeDtypeS...  35 us
    unnamed x17, local copies, waits for them, and re-layouts  5.48 us

profile of v1, /device:TPU:0, one launch (start us, length us, event | category | flops | bytes accessed | tf_op | source)
XLA Modules:
  0.0 40.5 jit_solution(17835891279200971114)
XLA Ops:
  0.0 0.0 copy-start.5
  0.0 0.0 copy-start.6
  0.0 0.0 copy-start.7
  0.0 0.6 %copy-done.5 = f32[8]{0:T(128)S(1)} copy-done((f32[8]{0:T(128)S(1)}, f32[8]{0:T(128)}, u32[]{:S(2)}) %copy-start.5) | copy-done | bytes 56
  0.7 0.0 copy-done.6
  0.7 0.0 copy-done.7
  0.7 0.0 copy-start
  0.7 1.0 %copy-done = f32[2,3,16,4,2,128]{5,4,3,2,1,0:T(2,128)S(1)} copy-done((f32[2,3,16,4,2,128]{5,4,3,2,1,0:T(2,128)S(1)}, f32[2,3,16,4,2,128]{5,4,3,2,1,0:T(2,128)}, u32[]{:S(2)}) %copy-start) | copy-done | bytes 393240
  1.7 0.0 copy-start.1
  1.7 1.0 %copy-done.1 = f32[2,3,16,4,2,128]{5,4,3,2,1,0:T(2,128)S(1)} copy-done((f32[2,3,16,4,2,128]{5,4,3,2,1,0:T(2,128)S(1)}, f32[2,3,16,4,2,128]{5,4,3,2,1,0:T(2,128)}, u32[]{:S(2)}) %copy-start.1) | copy-done | bytes 393240
  2.7 0.0 copy-start.2
  2.7 0.7 %copy-done.2 = s32[4,2,128]{2,1,0:T(2,128)S(1)} copy-done((s32[4,2,128]{2,1,0:T(2,128)S(1)}, s32[4,2,128]{2,1,0:T(2,128)}, u32[]{:S(2)}) %copy-start.2) | copy-done | bytes 4120
  3.4 0.0 copy-start.3
  3.4 0.7 %copy-done.3 = s32[4,2,128]{2,1,0:T(2,128)S(1)} copy-done((s32[4,2,128]{2,1,0:T(2,128)S(1)}, s32[4,2,128]{2,1,0:T(2,128)}, u32[]{:S(2)}) %copy-start.3) | copy-done | bytes 4120
  4.1 0.0 copy-start.4
  4.1 0.7 %copy-done.4 = f32[4,2,128]{2,1,0:T(2,128)S(1)} copy-done((f32[4,2,128]{2,1,0:T(2,128)S(1)}, f32[4,2,128]{2,1,0:T(2,128)}, u32[]{:S(2)}) %copy-start.4) | copy-done | bytes 4120
  4.7 35.0 %shard_map.82 = f32[768,128]{1,0:T(8,128)S(1)} custom-call(f32[8]{0:T(128)S(1)} %copy-done.5, f32[8]{0:T(128)S(1)} %copy-done.6, f32[8]{0:T(128)S(1)} %copy-done.7, s32[4,2,128]{2,1,0:T(2,128)S(1)} %copy-done.2, s32[4,2,128]{2,1,0:T(2,128)S(1)} %copy-done.3, f32[4,2,128]{2,1,0:T(2,128)S(1)} %copy-done.4, f32[768,128]{1,0:T(8,128)S(1)} %bitcast.4, ...), custom_call_target="tpu_custom_call" | custom-call | tf_op jit(solution)/shard_map/pallas_call | solution.py:405
  39.7 0.7 %copy.10 = f32[2,3,16,4,2,128]{5,4,3,2,1,0:T(2,128)} copy(f32[2,3,16,4,2,128]{5,4,3,2,1,0:T(2,128)S(1)} %bitcast.3) | data formatting | bytes 786432
Async XLA Ops:
  0.0 0.7 %copy-start.5 = (f32[8]{0:T(128)S(1)}, f32[8]{0:T(128)}, u32[]{:S(2)}) copy-start(f32[8]{0:T(128)} %lin_ref.1) | copy-start | bytes 100
  0.0 0.7 %copy-start.6 = (f32[8]{0:T(128)S(1)}, f32[8]{0:T(128)}, u32[]{:S(2)}) copy-start(f32[8]{0:T(128)} %loss_ref.1) | copy-start | bytes 100
  0.0 0.7 %copy-start.7 = (f32[8]{0:T(128)S(1)}, f32[8]{0:T(128)}, u32[]{:S(2)}) copy-start(f32[8]{0:T(128)} %kerr_ref.1) | copy-start | bytes 100
  0.7 1.0 %copy-start = (f32[2,3,16,4,2,128]{5,4,3,2,1,0:T(2,128)S(1)}, f32[2,3,16,4,2,128]{5,4,3,2,1,0:T(2,128)}, u32[]{:S(2)}) copy-start(f32[2,3,16,4,2,128]{5,4,3,2,1,0:T(2,128)} %param.8) | copy-start | bytes 1179652
  1.7 1.0 %copy-start.1 = (f32[2,3,16,4,2,128]{5,4,3,2,1,0:T(2,128)S(1)}, f32[2,3,16,4,2,128]{5,4,3,2,1,0:T(2,128)}, u32[]{:S(2)}) copy-start(f32[2,3,16,4,2,128]{5,4,3,2,1,0:T(2,128)} %param.9) | copy-start | bytes 1179652
  2.7 0.7 %copy-start.2 = (s32[4,2,128]{2,1,0:T(2,128)S(1)}, s32[4,2,128]{2,1,0:T(2,128)}, u32[]{:S(2)}) copy-start(s32[4,2,128]{2,1,0:T(2,128)} %region_ref.1) | copy-start | bytes 12292
  3.4 0.7 %copy-start.3 = (s32[4,2,128]{2,1,0:T(2,128)S(1)}, s32[4,2,128]{2,1,0:T(2,128)}, u32[]{:S(2)}) copy-start(s32[4,2,128]{2,1,0:T(2,128)} %mask_ref.1) | copy-start | bytes 12292
  4.1 0.7 %copy-start.4 = (f32[4,2,128]{2,1,0:T(2,128)S(1)}, f32[4,2,128]{2,1,0:T(2,128)}, u32[]{:S(2)}) copy-start(f32[4,2,128]{2,1,0:T(2,128)} %inten_ref.1) | copy-start | bytes 12292

commit v2 on v1

--- a/solution.py
+++ b/solution.py
@@ -28,13 +28,14 @@
 
 
 def kernel(
-    dims, lin_ref, loss_ref, kerr_ref, region_ref, mask_ref, inten_ref, rhs_ref, start_ref, out_ref,
+    dims, lin_ref, loss_ref, kerr_ref, region_hbm, mask_hbm, inten_hbm, rhs_hbm, start_hbm, pre_hbm, size_ref,
+    region_ref, mask_ref, inten_ref, rhs_ref, start_ref, out_ref, load_sem, known,
     field, resid, local, pre, cell, corner, corner_all, link, tips_out, tips_in, ends_out, ends_in, part,
     lat_parts, prop_parts,
     halo_send, halo_recv, corner_send, corner_recv, tips_send, tips_recv, ends_send, ends_recv,
     pre_send, pre_recv, lat_send, lat_recv, prop_send, prop_recv,
 ):
-    n, nl, S, Z, X, NY, u, m, rows = dims
+    n, nl, S, Z, X, NY, u, m, rows, together = dims
     NREG = lin_ref.shape[0]
     lat = lax.axis_index("lat")
     prop = lax.axis_index("prop")
@@ -53,8 +54,14 @@
             act(lax.rem(me + j, count))
             return carry
 
-        lax.fori_loop(1, count, body, 0)
-
+        lax.fori_loop(1, count, body, 0, unroll=True)
+
+    pairs = (
+        (start_hbm, start_ref), (region_hbm, region_ref), (mask_hbm, mask_ref), (inten_hbm, inten_ref), (rhs_hbm, rhs_ref)
+    )
+    loads = [pltpu.make_async_copy(src, dst, load_sem.at[i]) for i, (src, dst) in enumerate(pairs)]
+    for load in loads:
+        load.start()
     barrier = pltpu.get_barrier_semaphore()
 
     def greet(l, q):
@@ -62,13 +69,23 @@
 
     diag_up = jnp.logical_and(has_left, has_up)
     diag_down = jnp.logical_and(has_right, has_down)
-    others(n, prop, lambda q: greet(lat, q))
-    others(nl, lat, lambda l: greet(l, prop))
+    bits = [("lat", 1 << i) for i in range(nl.bit_length() - 1)] + [("prop", 1 << i) for i in range(n.bit_length() - 1)]
+
+    def facing(axis, bit):
+        return at(lat ^ bit, prop) if axis == "lat" else at(lat, prop ^ bit)
+
+    for axis, bit in bits:
+        pl.semaphore_signal(barrier, inc=1, device_id=facing(axis, bit), device_id_type=MESH)
+    pl.when(has_right)(lambda: greet(lat + 1, prop))
+    pl.when(has_left)(lambda: greet(lat - 1, prop))
+    pl.when(has_up)(lambda: greet(lat, prop + 1))
+    pl.when(has_down)(lambda: greet(lat, prop - 1))
     pl.when(diag_up)(lambda: greet(lat - 1, prop + 1))
     pl.when(diag_down)(lambda: greet(lat + 1, prop - 1))
 
     zero_plane = jnp.zeros((X, S, NY), jnp.float32)
     zero_line = jnp.zeros((S, NY), jnp.float32)
+    loads[0].wait()
     for c in range(2):
         for k in range(3):
             for z in range(Z):
@@ -96,6 +113,8 @@
     clear(jnp.logical_or(no_down, no_right), field, (0,), (X + 1,))
     clear(jnp.logical_or(no_up, no_left), field, (Z + 1,), (0,))
 
+    for load in loads[1:4]:
+        load.wait()
     region = region_ref[...]
     lin = jnp.zeros((Z, X, NY), jnp.float32)
     loss = lin
@@ -133,7 +152,9 @@
             corner[x, i : i + 1, :] = value[x : x + 1, :]
         corner[x, 6:8, :] = jnp.zeros((2, NY), jnp.float32)
 
-    count = (n - 1) + (nl - 1) + diag_up.astype(jnp.int32) + diag_down.astype(jnp.int32)
+    count = len(bits)
+    for cond in (has_right, has_left, has_up, has_down, diag_up, diag_down):
+        count = count + cond.astype(jnp.int32)
     pl.semaphore_wait(barrier, count)
 
     def remote(src, dst, send, recv, device):
@@ -159,9 +180,6 @@
 
     def corner_copy(q):
         return remote(corner.at[q // m], corner_all.at[prop], corner_send.at[q], corner_recv.at[prop], at_prop(q))
-
-    others(n, prop, lambda q: corner_copy(q).start())
-    corner_all[prop] = corner[prop // m]
 
     lane = lax.broadcasted_iota(jnp.int32, (X, S, NY), 2)
     at_first, at_last = lane == 0, lane == NY - 1
@@ -210,13 +228,32 @@
                     base = (c * 3 + k) * S * ZX + z * X + x
                     resid[c, k, z, x] = rhs_ref[pl.ds(base, S, stride=ZX), :] - parts[k][x]
 
+    def tell(i):
+        if i < len(bits):
+            pl.semaphore_signal(known.at[i], inc=1, device_id=facing(*bits[i]), device_id_type=MESH)
+
+    def hear(i):
+        if i < len(bits):
+            pl.semaphore_wait(known.at[i], 1)
+            tell(i + 1)
+
+    tell(1)
+    loads[4].wait()
     for i in (4, 5):
         pl.when(halos[i][2])(halos[i][0].wait_recv)
+    heard = 1
     for z in range(1, Z - 1):
+        hear(heard)
+        heard += 1
         residual(z)
+    hear(heard)
     for i in (0, 2):
         pl.when(halos[i][2])(halos[i][0].wait_recv)
     residual(0)
+    for i in range(heard + 1, len(bits)):
+        hear(i)
+    others(n, prop, lambda q: corner_copy(q).start())
+    corner_all[prop] = corner[prop // m]
     for i in (1, 3):
         pl.when(halos[i][2])(halos[i][0].wait_recv)
     if Z > 1:
@@ -340,6 +377,14 @@
     ]
     for copy, out, _ in sides:
         pl.when(out)(copy.start)
+    for c in range(2):
+        for k in range(3):
+            for z in range(Z):
+                for x in range(X):
+                    base = (c * 3 + k) * S * ZX + z * X + x
+                    out_ref[pl.ds(base, S, stride=ZX), :] = pre[c, k, z + 1, x + 1]
+    write = pltpu.make_async_copy(out_ref, pre_hbm, load_sem.at[0])
+    write.start()
     for copy, _, into in sides:
         pl.when(into)(copy.wait_recv)
 
@@ -372,18 +417,16 @@
             total = total + parts[j]
         return total
 
-    row = reduced(row, nl, lat, lat_parts, 0, lat_send, lat_recv, lambda l: at(l, prop))
-    row = reduced(row, n, prop, prop_parts, 1, prop_send, prop_recv, at_prop)
+    if together:
+        row = reduced(row, nl * n, lat * n + prop, prop_parts, 1, prop_send, prop_recv, lambda j: at(j // n, j % n))
+    else:
+        row = reduced(row, nl, lat, lat_parts, 0, lat_send, lat_recv, lambda l: at(l, prop))
+        row = reduced(row, n, prop, prop_parts, 1, prop_send, prop_recv, at_prop)
     wide = jnp.broadcast_to(row, (S, NY))
     cross_total = jnp.sum(jnp.where(on_cross, wide, 0.0), axis=1, keepdims=True)
     self_total = jnp.sum(jnp.where(on_self, wide, 0.0), axis=1, keepdims=True)
-    size = jnp.broadcast_to(cross_total / (self_total + tiny), (S, NY))
-    for c in range(2):
-        for k in range(3):
-            for z in range(Z):
-                for x in range(X):
-                    base = (c * 3 + k) * S * ZX + z * X + x
-                    out_ref[pl.ds(base, S, stride=ZX), :] = field[c, k, z + 1, x + 1] + size * pre[c, k, z + 1, x + 1]
+    size_ref[...] = jnp.broadcast_to(cross_total / (self_total + tiny), (S, NY))
+    write.wait()
     for copy, out, _ in halos + sides:
         pl.when(out)(copy.wait_send)
     others(n, prop, lambda q: corner_from(q).wait_send())
@@ -396,18 +439,28 @@
     m = n // X
     u = S // m
     rows = -(-12 * u // 8) * 8
-    dims = (n, nl, S, Z, X, NY, u, m, rows)
+    together = n * nl <= 64
+    team = n * nl if together else n
+    dims = (n, nl, S, Z, X, NY, u, m, rows, together)
     flat = (6 * S * Z * X, NY)
     f32 = jnp.float32
     vmem = pl.BlockSpec(memory_space=pltpu.VMEM)
     smem = pl.BlockSpec(memory_space=pltpu.SMEM)
     dma = pltpu.SemaphoreType.DMA
-    out = pl.pallas_call(
+    pre, size = pl.pallas_call(
         functools.partial(kernel, dims),
-        out_shape=jax.ShapeDtypeStruct(flat, f32),
-        in_specs=[smem] * 3 + [vmem] * 5,
-        out_specs=vmem,
+        out_shape=(jax.ShapeDtypeStruct(flat, f32), jax.ShapeDtypeStruct((S, NY), f32)),
+        in_specs=[smem] * 3 + [pl.BlockSpec(memory_space=pltpu.HBM)] * 5,
+        out_specs=(pl.BlockSpec(memory_space=pltpu.HBM), vmem),
         scratch_shapes=[
+            pltpu.VMEM(region.shape, region.dtype),
+            pltpu.VMEM(region.shape, core_mask.dtype),
+            pltpu.VMEM(region.shape, f32),
+            pltpu.VMEM(flat, f32),
+            pltpu.VMEM(flat, f32),
+            pltpu.VMEM(flat, f32),
+            dma((5,)),
+            pltpu.SemaphoreType.REGULAR((n.bit_length() + nl.bit_length(),)),
             pltpu.VMEM((2, 3, Z + 2, X + 2, S, NY), f32),
             pltpu.VMEM((2, 3, Z, X, S, NY), f32),
             pltpu.VMEM((2, 3, Z, X, S, NY), f32),
@@ -422,20 +475,20 @@
             pltpu.VMEM((n * rows, NY), f32),
             pltpu.VMEM((2, 1, NY), f32),
             pltpu.VMEM((nl, 1, NY), f32),
-            pltpu.VMEM((n, 1, NY), f32),
+            pltpu.VMEM((team, 1, NY), f32),
             dma((6,)), dma((6,)),
             dma((n,)), dma((n,)),
             dma((n,)), dma((n,)),
             dma((n,)), dma((n,)),
             dma((2,)), dma((2,)),
             dma((nl,)), dma((nl,)),
-            dma((n,)), dma((n,)),
+            dma((team,)), dma((team,)),
         ],
         compiler_params=pltpu.CompilerParams(
-            collective_id=0, has_side_effects=True, vmem_limit_bytes=32 * 1024 * 1024
+            collective_id=0, has_side_effects=True, vmem_limit_bytes=60 * 1024 * 1024
         ),
     )(eps_lin, eps_loss, kerr_coef, region, core_mask, intensity, right_side.reshape(flat), start_field.reshape(flat))
-    return out.reshape(right_side.shape)
+    return start_field + size.reshape(1, 1, S, 1, 1, NY) * pre.reshape(right_side.shape)
 
 
 def solution(mesh):

time: 40.8 us -> 35.5 us (0.87)
  local copies, waits for them, and re-layouts: 5.48 us -> 0.01 us
  other arithmetic: 0 us -> 1.96 us
  Pallas kernels: 35 us -> 33.4 us
    unnamed x17 -> x2, local copies, waits for them, and re-layouts: 5.48 us -> 0.01 us
    add x0 -> x1, other arithmetic: none -> 1.96 us  [per_device(): start_field + size.reshape(1, 1, S, 1, 1, NY) * pre.reshape(right_side.sh...]
    pallas_call x1, Pallas kernels: 35 us -> 33.4 us  [per_device(): pl.pallas_call(functools.partial(kernel, dims), out_shape=(jax.ShapeDtype...]
where the time goes in v2:
time: 35.5 us; the launch traced here: 35.3 us
  Pallas kernels  33.4 us (94%)
  other arithmetic  1.96 us (6%)
    pallas_call x1, Pallas kernels, per_device(): pl.pallas_call(functools.partial(kernel, dims), out_shape=(jax.ShapeDtype...  33.4 us
    add x1, other arithmetic, per_device(): start_field + size.reshape(1, 1, S, 1, 1, NY) * pre.reshape(right_side.sh...  1.96 us

profile of v2, /device:TPU:0, one launch (start us, length us, event | category | flops | bytes accessed | tf_op | source)
XLA Modules:
  0.0 35.3 jit_solution(18281789774545761352)
XLA Ops:
  0.0 0.0 copy-start
  0.0 33.4 %shard_map.82 = (f32[768,128]{1,0:T(8,128)}, f32[16,128]{1,0:T(8,128)}) custom-call(f32[8]{0:T(128)} %lin_ref.1, f32[8]{0:T(128)} %loss_ref.1, f32[8]{0:T(128)} %kerr_ref.1, s32[4,2,128]{2,1,0:T(2,128)} %region_hbm.1, s32[4,2,128]{2,1,0:T(2,128)} %mask_hbm.1, f32[4,2,128]{2,1,0:T(2,128)} %inten_hbm.1, f32[768,128]{1,0:T(8,128)} %bitcast.4, f32[768,128]{1,0:T(8,128)} %bitcast.3), custom_call_target="tpu_custom_call" | custom-call | tf_op jit(solution)/shard_map/pallas_call | solution.py:450
  33.4 0.0 copy-done
  33.4 2.0 %multiply_add_fusion = f32[2,3,16,4,2,128]{5,4,3,2,1,0:T(2,128)} fusion(f32[2,3,16,4,2,128]{5,4,3,2,1,0:T(2,128)S(1)} %copy-done, f32[2,3,16,4,2,128]{5,4,3,2,1,0:T(2,128)} %bitcast.5, f32[16,128]{1,0:T(8,128)} %get-tuple-element.7), kind=kLoop, calls=%fused_computation | loop fusion | flops 196608 | bytes 1187840 | tf_op jit(solution)/shard_map/add | solution.py:491
Async XLA Ops:
  0.0 33.4 %copy-start = (f32[2,3,16,4,2,128]{5,4,3,2,1,0:T(2,128)S(1)}, f32[2,3,16,4,2,128]{5,4,3,2,1,0:T(2,128)}, u32[]{:S(2)}) copy-start(f32[2,3,16,4,2,128]{5,4,3,2,1,0:T(2,128)} %param.9) | copy-start | bytes 1179652

commit v3 on v2

--- a/solution.py
+++ b/solution.py
@@ -28,14 +28,14 @@
 
 
 def kernel(
-    dims, lin_ref, loss_ref, kerr_ref, region_hbm, mask_hbm, inten_hbm, rhs_hbm, start_hbm, pre_hbm, size_ref,
-    region_ref, mask_ref, inten_ref, rhs_ref, start_ref, out_ref, load_sem, known,
+    dims, lin_ref, loss_ref, kerr_ref, region_hbm, mask_hbm, inten_hbm, rhs_hbm, start_hbm, out_ref, size_ref,
+    region_ref, mask_ref, inten_ref, rhs_ref, start_ref, load_sem, known,
     field, resid, local, pre, cell, corner, corner_all, link, tips_out, tips_in, ends_out, ends_in, part,
     lat_parts, prop_parts,
     halo_send, halo_recv, corner_send, corner_recv, tips_send, tips_recv, ends_send, ends_recv,
     pre_send, pre_recv, lat_send, lat_recv, prop_send, prop_recv,
 ):
-    n, nl, S, Z, X, NY, u, m, rows, together = dims
+    n, nl, S, Z, X, NY, ns, lo, u, m, rows, together = dims
     NREG = lin_ref.shape[0]
     lat = lax.axis_index("lat")
     prop = lax.axis_index("prop")
@@ -50,11 +50,8 @@
         return {"lat": l, "prop": q}
 
     def others(count, me, act):
-        def body(j, carry):
-            act(lax.rem(me + j, count))
-            return carry
-
-        lax.fori_loop(1, count, body, 0, unroll=True)
+        for j in range(count - 1, 0, -1):
+            act(me ^ j)
 
     pairs = (
         (start_hbm, start_ref), (region_hbm, region_ref), (mask_hbm, mask_ref), (inten_hbm, inten_ref), (rhs_hbm, rhs_ref)
@@ -112,6 +109,56 @@
     clear(no_up, field, (Z + 1,), inner_x)
     clear(jnp.logical_or(no_down, no_right), field, (0,), (X + 1,))
     clear(jnp.logical_or(no_up, no_left), field, (Z + 1,), (0,))
+
+    count = len(bits)
+    for cond in (has_right, has_left, has_up, has_down, diag_up, diag_down):
+        count = count + cond.astype(jnp.int32)
+    pl.semaphore_wait(barrier, count)
+
+    def remote(src, dst, send, recv, device):
+        return pltpu.make_async_remote_copy(
+            src_ref=src, dst_ref=dst, send_sem=send, recv_sem=recv, device_id=device, device_id_type=MESH
+        )
+
+    iz, ix = pl.ds(1, Z), pl.ds(1, X)
+    halo = [
+        (has_up, field.at[:, :, Z, ix], field.at[:, :, 0, ix], at(lat, prop + 1), has_down),
+        (has_down, field.at[:, 0:2, 1, ix], field.at[:, 0:2, Z + 1, ix], at(lat, prop - 1), has_up),
+        (diag_up, field.at[:, 2, Z, 1], field.at[:, 2, 0, X + 1], at(lat - 1, prop + 1), diag_down),
+        (diag_down, field.at[:, 0, 1, X], field.at[:, 0, Z + 1, 0], at(lat + 1, prop - 1), diag_up),
+        (has_right, field.at[:, :, iz, X], field.at[:, :, iz, 0], at(lat + 1, prop), has_left),
+        (has_left, field.at[:, 1:3, iz, 1], field.at[:, 1:3, iz, X + 1], at(lat - 1, prop), has_right),
+    ]
+    halos = [
+        (remote(src, dst, halo_send.at[i], halo_recv.at[i], device), out, into)
+        for i, (out, src, dst, device, into) in enumerate(halo)
+    ]
+    for copy, out, _ in halos:
+        pl.when(out)(copy.start)
+
+    mine = prop - lo
+    couples = jnp.logical_and(mine >= 0, mine < ns)
+    folded = lax.rem(mine + n, ns)
+
+    def couplers(act):
+        for j in range(ns - 1, 0, -1):
+            act(folded ^ j)
+        if ns < n:
+            pl.when(jnp.logical_not(couples))(lambda: act(folded))
+
+    def corner_copy(t):
+        return remote(corner.at[t // m], corner_all.at[prop], corner_send.at[t], corner_recv.at[prop], at_prop(t + lo))
+
+    def tell(i):
+        if i < len(bits):
+            pl.semaphore_signal(known.at[i], inc=1, device_id=facing(*bits[i]), device_id_type=MESH)
+
+    def hear(i):
+        if i < len(bits):
+            pl.semaphore_wait(known.at[i], 1)
+            tell(i + 1)
+
+    tell(1)
 
     for load in loads[1:4]:
         load.wait()
@@ -152,35 +199,6 @@
             corner[x, i : i + 1, :] = value[x : x + 1, :]
         corner[x, 6:8, :] = jnp.zeros((2, NY), jnp.float32)
 
-    count = len(bits)
-    for cond in (has_right, has_left, has_up, has_down, diag_up, diag_down):
-        count = count + cond.astype(jnp.int32)
-    pl.semaphore_wait(barrier, count)
-
-    def remote(src, dst, send, recv, device):
-        return pltpu.make_async_remote_copy(
-            src_ref=src, dst_ref=dst, send_sem=send, recv_sem=recv, device_id=device, device_id_type=MESH
-        )
-
-    iz, ix = pl.ds(1, Z), pl.ds(1, X)
-    halo = [
-        (has_up, field.at[:, :, Z, ix], field.at[:, :, 0, ix], at(lat, prop + 1), has_down),
-        (has_down, field.at[:, 0:2, 1, ix], field.at[:, 0:2, Z + 1, ix], at(lat, prop - 1), has_up),
-        (diag_up, field.at[:, 2, Z, 1], field.at[:, 2, 0, X + 1], at(lat - 1, prop + 1), diag_down),
-        (diag_down, field.at[:, 0, 1, X], field.at[:, 0, Z + 1, 0], at(lat + 1, prop - 1), diag_up),
-        (has_right, field.at[:, :, iz, X], field.at[:, :, iz, 0], at(lat + 1, prop), has_left),
-        (has_left, field.at[:, 1:3, iz, 1], field.at[:, 1:3, iz, X + 1], at(lat - 1, prop), has_right),
-    ]
-    halos = [
-        (remote(src, dst, halo_send.at[i], halo_recv.at[i], device), out, into)
-        for i, (out, src, dst, device, into) in enumerate(halo)
-    ]
-    for copy, out, _ in halos:
-        pl.when(out)(copy.start)
-
-    def corner_copy(q):
-        return remote(corner.at[q // m], corner_all.at[prop], corner_send.at[q], corner_recv.at[prop], at_prop(q))
-
     lane = lax.broadcasted_iota(jnp.int32, (X, S, NY), 2)
     at_first, at_last = lane == 0, lane == NY - 1
 
@@ -228,16 +246,6 @@
                     base = (c * 3 + k) * S * ZX + z * X + x
                     resid[c, k, z, x] = rhs_ref[pl.ds(base, S, stride=ZX), :] - parts[k][x]
 
-    def tell(i):
-        if i < len(bits):
-            pl.semaphore_signal(known.at[i], inc=1, device_id=facing(*bits[i]), device_id_type=MESH)
-
-    def hear(i):
-        if i < len(bits):
-            pl.semaphore_wait(known.at[i], 1)
-            tell(i + 1)
-
-    tell(1)
     loads[4].wait()
     for i in (4, 5):
         pl.when(halos[i][2])(halos[i][0].wait_recv)
@@ -252,8 +260,7 @@
     residual(0)
     for i in range(heard + 1, len(bits)):
         hear(i)
-    others(n, prop, lambda q: corner_copy(q).start())
-    corner_all[prop] = corner[prop // m]
+    couplers(lambda t: corner_copy(t).start())
     for i in (1, 3):
         pl.when(halos[i][2])(halos[i][0].wait_recv)
     if Z > 1:
@@ -289,70 +296,74 @@
     def block(q):
         return pl.ds(pl.multiple_of(q * rows, 8), rows)
 
-    def tips_copy(q):
-        return remote(tips_out.at[block(q)], tips_in.at[block(prop)], tips_send.at[q], tips_recv.at[prop], at_prop(q))
-
-    others(n, prop, lambda q: tips_copy(q).start())
-    tips_in[block(prop), :] = tips_out[block(prop), :]
+    def tips_copy(t):
+        return remote(tips_out.at[block(t)], tips_in.at[block(prop)], tips_send.at[t], tips_recv.at[prop], at_prop(t + lo))
+
+    def tips_from(q):
+        return remote(tips_out.at[block(0)], tips_in.at[block(q)], tips_send.at[0], tips_recv.at[q], at_prop(q))
 
     def corner_from(q):
-        return remote(corner.at[q // m], corner_all.at[q], corner_send.at[q], corner_recv.at[q], at_prop(q))
-
-    others(n, prop, lambda q: corner_from(q).wait_recv())
-    beta = (jnp.zeros((1, NY), jnp.float32),) * 2
-
-    def link_step(k, beta):
-        first, cross, last = [(corner_all[k, 2 * i : 2 * i + 1, :], corner_all[k, 2 * i + 1 : 2 * i + 2, :]) for i in range(3)]
-        fb = cmul(first, beta)
-        gamma = cinv((1.0 - fb[0], -fb[1]))
-        carry = cmul(cross, gamma)
-        mix = cmul(carry, beta)
-        for i, value in enumerate((*carry, *mix, *gamma, *cmul(gamma, first), *beta)):
-            link[k, i] = value
-        return cadd(last, cmul(cross, mix))
-
-    for k in range(n):
-        beta = link_step(k, beta)
-
-    def tips_from(q):
-        return remote(tips_out.at[block(q)], tips_in.at[block(q)], tips_send.at[q], tips_recv.at[q], at_prop(q))
-
-    others(n, prop, lambda q: tips_from(q).wait_recv())
-    span = 3 * u
-
-    def linked(k, i):
-        return (link[k, 2 * i], link[k, 2 * i + 1])
-
-    def tip(k, b):
-        return tuple(tips_in[k * rows + (b * 2 + c) * span : k * rows + (b * 2 + c + 1) * span, :] for c in range(2))
-
-    def put(k, b, value):
-        for c in range(2):
-            ends_out[k * rows + (b * 2 + c) * span : k * rows + (b * 2 + c + 1) * span, :] = value[c]
-
-    none = (jnp.zeros((span, NY), jnp.float32),) * 2
-    alphas = [none]
-    for k in range(n):
-        alphas.append(
-            cadd(cadd(tip(k, 1), cmul(linked(k, 1), tip(k, 0))), cmul(linked(k, 0), alphas[-1]))
-        )
-    first = none
-    for k in range(n - 1, -1, -1):
-        put(k, 1, first)
-        source = cadd(cmul(linked(k, 2), tip(k, 0)), cmul(linked(k, 3), alphas[k]))
-        first = cadd(source, cmul(linked(k, 0), first))
-        put(k, 0, cadd(alphas[k], cmul(linked(k, 4), first)) if k else none)
+        return remote(corner.at[0], corner_all.at[q], corner_send.at[0], corner_recv.at[q], at_prop(q))
 
     def ends_copy(q):
-        return remote(ends_out.at[block(q)], ends_in.at[block(prop)], ends_send.at[q], ends_recv.at[prop], at_prop(q))
-
-    def ends_from(q):
-        return remote(ends_out.at[block(q)], ends_in.at[block(q)], ends_send.at[q], ends_recv.at[q], at_prop(q))
-
-    others(n, prop, lambda q: ends_copy(q).start())
-    ends_in[block(prop), :] = ends_out[block(prop), :]
-    others(n, prop, lambda q: ends_from(q).wait_recv())
-
+        return remote(ends_out.at[block(q)], ends_in.at[block(mine)], ends_send.at[q], ends_recv.at[mine], at_prop(q))
+
+    def ends_from(t):
+        return remote(ends_out.at[block(0)], ends_in.at[block(t)], ends_send.at[0], ends_recv.at[t], at_prop(t + lo))
+
+    couplers(lambda t: tips_copy(t).start())
+
+    def couple():
+        tips_in[block(prop), :] = tips_out[block(mine), :]
+        corner_all[prop] = corner[mine // m]
+        others(n, prop, lambda q: corner_from(q).wait_recv())
+        beta = (jnp.zeros((1, NY), jnp.float32),) * 2
+
+        def link_step(k, beta):
+            first, cross, last = [(corner_all[k, 2 * i : 2 * i + 1, :], corner_all[k, 2 * i + 1 : 2 * i + 2, :]) for i in range(3)]
+            fb = cmul(first, beta)
+            gamma = cinv((1.0 - fb[0], -fb[1]))
+            carry = cmul(cross, gamma)
+            mix = cmul(carry, beta)
+            for i, value in enumerate((*carry, *mix, *gamma, *cmul(gamma, first), *beta)):
+                link[k, i] = value
+            return cadd(last, cmul(cross, mix))
+
+        for k in range(n):
+            beta = link_step(k, beta)
+
+        others(n, prop, lambda q: tips_from(q).wait_recv())
+        span = 3 * u
+
+        def linked(k, i):
+            return (link[k, 2 * i], link[k, 2 * i + 1])
+
+        def tip(k, b):
+            return tuple(tips_in[k * rows + (b * 2 + c) * span : k * rows + (b * 2 + c + 1) * span, :] for c in range(2))
+
+        def put(k, b, value):
+            for c in range(2):
+                ends_out[k * rows + (b * 2 + c) * span : k * rows + (b * 2 + c + 1) * span, :] = value[c]
+
+        none = (jnp.zeros((span, NY), jnp.float32),) * 2
+        alphas = [none]
+        for k in range(n):
+            alphas.append(
+                cadd(cadd(tip(k, 1), cmul(linked(k, 1), tip(k, 0))), cmul(linked(k, 0), alphas[-1]))
+            )
+        first = none
+        for k in range(n - 1, -1, -1):
+            put(k, 1, first)
+            source = cadd(cmul(linked(k, 2), tip(k, 0)), cmul(linked(k, 3), alphas[k]))
+            first = cadd(source, cmul(linked(k, 0), first))
+            put(k, 0, cadd(alphas[k], cmul(linked(k, 4), first)) if k else none)
+
+        others(n, prop, lambda q: ends_copy(q).start())
+        ends_in[block(mine), :] = ends_out[block(prop), :]
+
+    pl.when(couples)(couple)
+
+    couplers(lambda t: ends_from(t).wait_recv())
     for k in range(3):
         sides = []
         for b in range(2):
@@ -383,8 +394,6 @@
                 for x in range(X):
                     base = (c * 3 + k) * S * ZX + z * X + x
                     out_ref[pl.ds(base, S, stride=ZX), :] = pre[c, k, z + 1, x + 1]
-    write = pltpu.make_async_copy(out_ref, pre_hbm, load_sem.at[0])
-    write.start()
     for copy, _, into in sides:
         pl.when(into)(copy.wait_recv)
 
@@ -426,22 +435,23 @@
     cross_total = jnp.sum(jnp.where(on_cross, wide, 0.0), axis=1, keepdims=True)
     self_total = jnp.sum(jnp.where(on_self, wide, 0.0), axis=1, keepdims=True)
     size_ref[...] = jnp.broadcast_to(cross_total / (self_total + tiny), (S, NY))
-    write.wait()
     for copy, out, _ in halos + sides:
         pl.when(out)(copy.wait_send)
-    others(n, prop, lambda q: corner_from(q).wait_send())
-    others(n, prop, lambda q: tips_from(q).wait_send())
-    others(n, prop, lambda q: ends_from(q).wait_send())
+    couplers(lambda t: corner_copy(t).wait_send())
+    couplers(lambda t: tips_copy(t).wait_send())
+    pl.when(couples)(lambda: others(n, prop, lambda q: ends_copy(q).wait_send()))
 
 
 def per_device(n, nl, right_side, start_field, region, core_mask, intensity, eps_lin, eps_loss, kerr_coef):
     S, Z, X, NY = right_side.shape[2:]
-    m = n // X
+    ns = n
+    lo = (n - ns) // 2
+    m = ns // X
     u = S // m
     rows = -(-12 * u // 8) * 8
     together = n * nl <= 64
     team = n * nl if together else n
-    dims = (n, nl, S, Z, X, NY, u, m, rows, together)
+    dims = (n, nl, S, Z, X, NY, ns, lo, u, m, rows, together)
     flat = (6 * S * Z * X, NY)
     f32 = jnp.float32
     vmem = pl.BlockSpec(memory_space=pltpu.VMEM)
@@ -449,14 +459,13 @@
     dma = pltpu.SemaphoreType.DMA
     pre, size = pl.pallas_call(
         functools.partial(kernel, dims),
-        out_shape=(jax.ShapeDtypeStruct(flat, f32), jax.ShapeDtypeStruct((S, NY), f32)),
+        out_shape=(pltpu.VMEM(flat, f32), pltpu.VMEM((S, NY), f32)),
         in_specs=[smem] * 3 + [pl.BlockSpec(memory_space=pltpu.HBM)] * 5,
-        out_specs=(pl.BlockSpec(memory_space=pltpu.HBM), vmem),
+        out_specs=(vmem, vmem),
         scratch_shapes=[
             pltpu.VMEM(region.shape, region.dtype),
             pltpu.VMEM(region.shape, core_mask.dtype),
             pltpu.VMEM(region.shape, f32),
-            pltpu.VMEM(flat, f32),
             pltpu.VMEM(flat, f32),
             pltpu.VMEM(flat, f32),
             dma((5,)),
@@ -469,10 +478,10 @@
             pltpu.VMEM((X, 8, NY), f32),
             pltpu.VMEM((n, 8, NY), f32),
             pltpu.VMEM((n, 10, 1, NY), f32),
+            pltpu.VMEM((ns * rows, NY), f32),
             pltpu.VMEM((n * rows, NY), f32),
             pltpu.VMEM((n * rows, NY), f32),
-            pltpu.VMEM((n * rows, NY), f32),
-            pltpu.VMEM((n * rows, NY), f32),
+            pltpu.VMEM((ns * rows, NY), f32),
             pltpu.VMEM((2, 1, NY), f32),
             pltpu.VMEM((nl, 1, NY), f32),
             pltpu.VMEM((team, 1, NY), f32),
@@ -488,7 +497,9 @@
             collective_id=0, has_side_effects=True, vmem_limit_bytes=60 * 1024 * 1024
         ),
     )(eps_lin, eps_loss, kerr_coef, region, core_mask, intensity, right_side.reshape(flat), start_field.reshape(flat))
-    return start_field + size.reshape(1, 1, S, 1, 1, NY) * pre.reshape(right_side.shape)
+    tiled = (6, S, Z * X, NY)
+    new = start_field.reshape(tiled) + size.reshape(1, S, 1, NY) * pre.reshape(tiled)
+    return new.reshape(right_side.shape)
 
 
 def solution(mesh):

time: 35.5 us -> 33.2 us (0.935)
  Pallas kernels: 33.4 us -> 32 us
  other arithmetic: 1.96 us -> 0.96 us
    pallas_call x1, Pallas kernels: 33.4 us -> 32 us  [per_device(): pl.pallas_call(functools.partial(kernel, dims), out_shape=(pltpu.VMEM(fla...]
    add x1, other arithmetic: 1.96 us -> 0.96 us  [per_device(): start_field.reshape(tiled) + size.reshape(1, S, 1, NY) * pre.reshape(tiled)]
where the time goes in v3:
time: 33.2 us; the launch traced here: 33 us
  Pallas kernels  32 us (96%)
  other arithmetic  0.96 us (3%)
    pallas_call x1, Pallas kernels, per_device(): pl.pallas_call(functools.partial(kernel, dims), out_shape=(pltpu.VMEM(fla...  32 us
    add x1, other arithmetic, per_device(): start_field.reshape(tiled) + size.reshape(1, S, 1, NY) * pre.reshape(tiled)  0.96 us

profile of v3, /device:TPU:0, one launch (start us, length us, event | category | flops | bytes accessed | tf_op | source)
XLA Modules:
  0.0 33.0 jit_solution(15784745285975150742)
XLA Ops:
  0.0 0.0 copy-start
  0.0 32.0 %shard_map.82 = (f32[768,128]{1,0:T(8,128)S(1)}, f32[16,128]{1,0:T(8,128)S(1)}) custom-call(f32[8]{0:T(128)} %lin_ref.1, f32[8]{0:T(128)} %loss_ref.1, f32[8]{0:T(128)} %kerr_ref.1, s32[4,2,128]{2,1,0:T(2,128)} %region_hbm.1, s32[4,2,128]{2,1,0:T(2,128)} %mask_hbm.1, f32[4,2,128]{2,1,0:T(2,128)} %inten_hbm.1, f32[768,128]{1,0:T(8,128)} %bitcast.5, ...), custom_call_target="tpu_custom_call" | custom-call | tf_op jit(solution)/shard_map/pallas_call | solution.py:460
  32.1 0.0 copy-done
  32.1 1.0 %multiply_add_fusion = f32[2,3,16,4,2,128]{5,4,3,2,1,0:T(2,128)} fusion(f32[2,3,16,4,2,128]{5,4,3,2,1,0:T(2,128)S(1)} %copy-done, f32[2,3,16,4,2,128]{5,4,3,2,1,0:T(2,128)S(1)} %bitcast.3, f32[16,128]{1,0:T(8,128)S(1)} %get-tuple-element.7), kind=kLoop, calls=%fused_computation | loop fusion | flops 196608 | bytes 1187840 | tf_op jit(solution)/shard_map/add | solution.py:501
Async XLA Ops:
  0.0 32.1 %copy-start = (f32[2,3,16,4,2,128]{5,4,3,2,1,0:T(2,128)S(1)}, f32[2,3,16,4,2,128]{5,4,3,2,1,0:T(2,128)}, u32[]{:S(2)}) copy-start(f32[2,3,16,4,2,128]{5,4,3,2,1,0:T(2,128)} %param.9) | copy-start | bytes 1179652

commit v4 on v3

--- a/solution.py
+++ b/solution.py
@@ -28,7 +28,7 @@
 
 
 def kernel(
-    dims, lin_ref, loss_ref, kerr_ref, region_hbm, mask_hbm, inten_hbm, rhs_hbm, start_hbm, out_ref, size_ref,
+    dims, lin_ref, loss_ref, kerr_ref, region_hbm, mask_hbm, inten_hbm, rhs_hbm, start_hbm, out_ref,
     region_ref, mask_ref, inten_ref, rhs_ref, start_ref, load_sem, known,
     field, resid, local, pre, cell, corner, corner_all, link, tips_out, tips_in, ends_out, ends_in, part,
     lat_parts, prop_parts,
@@ -119,6 +119,9 @@
         return pltpu.make_async_remote_copy(
             src_ref=src, dst_ref=dst, send_sem=send, recv_sem=recv, device_id=device, device_id_type=MESH
         )
+
+    def whole(ref, sem):
+        pltpu.make_async_copy(ref, ref, sem).wait()
 
     iz, ix = pl.ds(1, Z), pl.ds(1, X)
     halo = [
@@ -147,7 +150,7 @@
             pl.when(jnp.logical_not(couples))(lambda: act(folded))
 
     def corner_copy(t):
-        return remote(corner.at[t // m], corner_all.at[prop], corner_send.at[t], corner_recv.at[prop], at_prop(t + lo))
+        return remote(corner.at[t // m], corner_all.at[prop], corner_send.at[0], corner_recv.at[0], at_prop(t + lo))
 
     def tell(i):
         if i < len(bits):
@@ -297,7 +300,7 @@
         return pl.ds(pl.multiple_of(q * rows, 8), rows)
 
     def tips_copy(t):
-        return remote(tips_out.at[block(t)], tips_in.at[block(prop)], tips_send.at[t], tips_recv.at[prop], at_prop(t + lo))
+        return remote(tips_out.at[block(t)], tips_in.at[block(prop)], tips_send.at[0], tips_recv.at[0], at_prop(t + lo))
 
     def tips_from(q):
         return remote(tips_out.at[block(0)], tips_in.at[block(q)], tips_send.at[0], tips_recv.at[q], at_prop(q))
@@ -306,7 +309,7 @@
         return remote(corner.at[0], corner_all.at[q], corner_send.at[0], corner_recv.at[q], at_prop(q))
 
     def ends_copy(q):
-        return remote(ends_out.at[block(q)], ends_in.at[block(mine)], ends_send.at[q], ends_recv.at[mine], at_prop(q))
+        return remote(ends_out.at[block(q)], ends_in.at[block(mine)], ends_send.at[0], ends_recv.at[0], at_prop(q))
 
     def ends_from(t):
         return remote(ends_out.at[block(0)], ends_in.at[block(t)], ends_send.at[0], ends_recv.at[t], at_prop(t + lo))
@@ -316,7 +319,7 @@
     def couple():
         tips_in[block(prop), :] = tips_out[block(mine), :]
         corner_all[prop] = corner[mine // m]
-        others(n, prop, lambda q: corner_from(q).wait_recv())
+        whole(corner_all.at[pl.ds(0, n - 1)], corner_recv.at[0])
         beta = (jnp.zeros((1, NY), jnp.float32),) * 2
 
         def link_step(k, beta):
@@ -332,7 +335,7 @@
         for k in range(n):
             beta = link_step(k, beta)
 
-        others(n, prop, lambda q: tips_from(q).wait_recv())
+        whole(tips_in.at[pl.ds(0, (n - 1) * rows)], tips_recv.at[0])
         span = 3 * u
 
         def linked(k, i):
@@ -363,7 +366,7 @@
 
     pl.when(couples)(couple)
 
-    couplers(lambda t: ends_from(t).wait_recv())
+    whole(ends_in.at[pl.ds(0, (n - 1) * rows)], ends_recv.at[0])
     for k in range(3):
         sides = []
         for b in range(2):
@@ -388,12 +391,6 @@
     ]
     for copy, out, _ in sides:
         pl.when(out)(copy.start)
-    for c in range(2):
-        for k in range(3):
-            for z in range(Z):
-                for x in range(X):
-                    base = (c * 3 + k) * S * ZX + z * X + x
-                    out_ref[pl.ds(base, S, stride=ZX), :] = pre[c, k, z + 1, x + 1]
     for copy, _, into in sides:
         pl.when(into)(copy.wait_recv)
 
@@ -416,11 +413,11 @@
         parts[me] = row
 
         def copy(q, own):
-            return remote(part.at[i], parts.at[own], send.at[q], recv.at[own], device(q))
+            return remote(part.at[i], parts.at[own], send.at[0], recv.at[0], device(q))
 
         others(count, me, lambda q: copy(q, me).start())
-        others(count, me, lambda q: copy(q, q).wait_recv())
-        others(count, me, lambda q: copy(q, q).wait_send())
+        whole(parts.at[pl.ds(0, count - 1)], recv.at[0])
+        whole(parts.at[pl.ds(0, count - 1)], send.at[0])
         total = parts[0]
         for j in range(1, count):
             total = total + parts[j]
@@ -434,12 +431,18 @@
     wide = jnp.broadcast_to(row, (S, NY))
     cross_total = jnp.sum(jnp.where(on_cross, wide, 0.0), axis=1, keepdims=True)
     self_total = jnp.sum(jnp.where(on_self, wide, 0.0), axis=1, keepdims=True)
-    size_ref[...] = jnp.broadcast_to(cross_total / (self_total + tiny), (S, NY))
+    size = jnp.broadcast_to(cross_total / (self_total + tiny), (S, NY))
+    for c in range(2):
+        for k in range(3):
+            for z in range(Z):
+                for x in range(X):
+                    base = (c * 3 + k) * S * ZX + z * X + x
+                    out_ref[pl.ds(base, S, stride=ZX), :] = field[c, k, z + 1, x + 1] + size * pre[c, k, z + 1, x + 1]
     for copy, out, _ in halos + sides:
         pl.when(out)(copy.wait_send)
-    couplers(lambda t: corner_copy(t).wait_send())
-    couplers(lambda t: tips_copy(t).wait_send())
-    pl.when(couples)(lambda: others(n, prop, lambda q: ends_copy(q).wait_send()))
+    whole(corner_all.at[pl.ds(0, n - 1)], corner_send.at[0])
+    whole(tips_in.at[pl.ds(0, (n - 1) * rows)], tips_send.at[0])
+    whole(ends_in.at[pl.ds(0, (n - 1) * rows)], ends_send.at[0])
 
 
 def per_device(n, nl, right_side, start_field, region, core_mask, intensity, eps_lin, eps_loss, kerr_coef):
@@ -457,11 +460,11 @@
     vmem = pl.BlockSpec(memory_space=pltpu.VMEM)
     smem = pl.BlockSpec(memory_space=pltpu.SMEM)
     dma = pltpu.SemaphoreType.DMA
-    pre, size = pl.pallas_call(
+    new = pl.pallas_call(
         functools.partial(kernel, dims),
-        out_shape=(pltpu.VMEM(flat, f32), pltpu.VMEM((S, NY), f32)),
+        out_shape=pltpu.VMEM(flat, f32),
         in_specs=[smem] * 3 + [pl.BlockSpec(memory_space=pltpu.HBM)] * 5,
-        out_specs=(vmem, vmem),
+        out_specs=vmem,
         scratch_shapes=[
             pltpu.VMEM(region.shape, region.dtype),
             pltpu.VMEM(region.shape, core_mask.dtype),
@@ -497,8 +500,6 @@
             collective_id=0, has_side_effects=True, vmem_limit_bytes=60 * 1024 * 1024
         ),
     )(eps_lin, eps_loss, kerr_coef, region, core_mask, intensity, right_side.reshape(flat), start_field.reshape(flat))
-    tiled = (6, S, Z * X, NY)
-    new = start_field.reshape(tiled) + size.reshape(1, S, 1, NY) * pre.reshape(tiled)
     return new.reshape(right_side.shape)
 
 

time: 33.2 us -> 32.7 us (0.985)
  other arithmetic: 0.96 us -> 0 us
  local copies, waits for them, and re-layouts: 0.01 us -> 0.75 us
    add x1 -> x0, other arithmetic: 0.96 us -> none  [per_device(): start_field.reshape(tiled) + size.reshape(1, S, 1, NY) * pre.reshape(tiled)]
    unnamed x2 -> x1, local copies, waits for them, and re-layouts: 0.01 us -> 0.75 us
where the time goes in v4:
time: 32.7 us; the launch traced here: 32.5 us
  Pallas kernels  31.8 us (97%)
  local copies, waits for them, and re-layouts  0.75 us (2%)
    pallas_call x1, Pallas kernels, per_device(): pl.pallas_call(functools.partial(kernel, dims), out_shape=pltpu.VMEM(flat...  31.8 us
    unnamed x1, local copies, waits for them, and re-layouts  0.75 us

profile of v4, /device:TPU:0, one launch (start us, length us, event | category | flops | bytes accessed | tf_op | source)
XLA Modules:
  0.0 32.5 jit_solution(11936024350792059268)
XLA Ops:
  0.0 31.8 %shard_map.82 = f32[768,128]{1,0:T(8,128)S(1)} custom-call(f32[8]{0:T(128)} %lin_ref.1, f32[8]{0:T(128)} %loss_ref.1, f32[8]{0:T(128)} %kerr_ref.1, s32[4,2,128]{2,1,0:T(2,128)} %region_hbm.1, s32[4,2,128]{2,1,0:T(2,128)} %mask_hbm.1, f32[4,2,128]{2,1,0:T(2,128)} %inten_hbm.1, f32[768,128]{1,0:T(8,128)} %bitcast.4, f32[768,128]{1,0:T(8,128)} %bitcast.5), custom_call_target="tpu_custom_call" | custom-call | tf_op jit(solution)/shard_map/pallas_call | solution.py:463
  31.8 0.7 %copy.10 = f32[2,3,16,4,2,128]{5,4,3,2,1,0:T(2,128)} copy(f32[2,3,16,4,2,128]{5,4,3,2,1,0:T(2,128)S(1)} %bitcast.3) | data formatting | bytes 786432
